TPU v7x, 32 devices: a whole 2x2x4 slice. The times are simulated.
32 devices in a mesh: fsdp: 4 (over z), ctx: 4 (over y, core), tp: 2 (over x).
Axes of the slice: x: 2, y: 2, z: 4, core: 2. Of those that a mesh axis runs over, the one named last changes fastest.
Arguments:
- layer_input: bfloat16 [4, 2048, 768], P('fsdp', 'ctx'), may hold values from -6 to 6
- cotangent: bfloat16 [4, 2048, 768], P('fsdp', 'ctx'), may hold values from -6 to 6
- segments: int32 [4, 2048], P('fsdp'), may hold values from 0 to 2047, as said below
- slot_order: int32 [4, 8], P('fsdp'), may hold values from 0 to 7, as said below
- first_gain: bfloat16 [768], P(('fsdp', 'ctx')), may hold values from 0.25 to 1.75
- first_shift: bfloat16 [768], P(('fsdp', 'ctx')), may hold values from -3 to 3
- project_weight: bfloat16 [768, 3, 768], P(('fsdp', 'ctx'), None, 'tp'), may hold values from -0.21875 to 0.21875
- project_bias: bfloat16 [2, 768], P(None, 'tp'), may hold values from -4 to 4
- output_weight: bfloat16 [768, 768], P('tp', ('fsdp', 'ctx')), may hold values from -1.5 to 1.5
- output_bias: bfloat16 [768], P(('fsdp', 'ctx')), may hold values from -3 to 3
- second_gain: bfloat16 [768], P(('fsdp', 'ctx')), may hold values from 0.25 to 1.75
- second_shift: bfloat16 [768], P(('fsdp', 'ctx')), may hold values from -3 to 3
- expand_weight: bfloat16 [768, 3072], P(('fsdp', 'ctx'), 'tp'), may hold values from -0.21875 to 0.21875
- expand_bias: bfloat16 [3072], P('tp'), may hold values from -4 to 4
- shrink_weight: bfloat16 [3072, 768], P('tp', ('fsdp', 'ctx')), may hold values from -0.109375 to 0.109375
- shrink_bias: bfloat16 [768], P(('fsdp', 'ctx')), may hold values from -3 to 3
Outputs:
- layer_output: bfloat16 [4, 2048, 768], P('fsdp', 'ctx')
- input_delta: float32 [4, 2048, 768], P('fsdp', 'ctx')
- first_gain_delta: float32 [768], P(('fsdp', 'ctx'))
- first_shift_delta: float32 [768], P(('fsdp', 'ctx'))
- project_weight_delta: float32 [768, 3, 768], P(('fsdp', 'ctx'), None, 'tp')
- project_bias_delta: float32 [2, 768], P(None, 'tp')
- output_weight_delta: float32 [768, 768], P('tp', ('fsdp', 'ctx'))
- output_bias_delta: float32 [768], P(('fsdp', 'ctx'))
- second_gain_delta: float32 [768], P(('fsdp', 'ctx'))
- second_shift_delta: float32 [768], P(('fsdp', 'ctx'))
- expand_weight_delta: float32 [768, 3072], P(('fsdp', 'ctx'), 'tp')
- expand_bias_delta: float32 [3072], P('tp')
- shrink_weight_delta: float32 [3072, 768], P('tp', ('fsdp', 'ctx'))
- shrink_bias_delta: float32 [768], P(('fsdp', 'ctx'))
Inputs may be any that keep to these rules, and one draw needn't show every extreme that they name: `segments`: taken in the order of positions (slot s of a sequence holds the 256 positions from slot_order[s] * 256 on), the sequence is cut into documents that follow one another; every token's segment number is the position of its document's last token; a document spans at most 800 positions and at least 60 unless it ends its sequence; every sequence has one document of exactly 800. `slot_order`: each row is a permutation.
All inputs are finite; a program needn't handle non-finite values.
Results may differ from a plain program's by a relative error of at most 0.02.
Values may be sent and summed in bfloat16 or wider, within the bound.
A program may use at most 128 MiB of HBM per device.

v0:
```python
from functools import partial

import jax
import jax.numpy as jnp
from jax import lax
from jax.sharding import PartitionSpec as P

HEAD_DIM = 64


EPSILON = 1e-05
SCALE = 0.125
NEGATIVE = -1000000000.0
TILE = 512


def contract_rows(left, right):
    return lax.dot_general(
        left, right, (((0,), (0,)), ((), ())), preferred_element_type=jnp.float32
    )


def times_transpose(left, right):
    return lax.dot_general(
        left, right, (((1,), (1,)), ((), ())), preferred_element_type=jnp.float32
    )


def normalize_parts(rows):
    mean = jnp.mean(rows, axis=-1, keepdims=True)
    centred = rows - mean
    spread = jnp.mean(centred * centred, axis=-1, keepdims=True)
    inverse = lax.rsqrt(spread + EPSILON)
    return (centred * inverse, inverse)


def norm_backward(upstream, unit, inverse, gain):
    scaled = upstream * gain
    back = inverse * (
        scaled
        - jnp.mean(scaled, axis=-1, keepdims=True)
        - unit * jnp.mean(scaled * unit, axis=-1, keepdims=True)
    )
    return (back, jnp.sum(upstream * unit, axis=0), jnp.sum(upstream, axis=0))


def split_pairs(array, pairs):
    seqs, count, width = array.shape
    span = width // pairs
    return (
        array.reshape(seqs, count, pairs, span)
        .transpose(0, 2, 1, 3)
        .reshape(seqs * pairs, count, span)
    )


def join_pairs(array, seqs):
    items, count, span = array.shape
    pairs = items // seqs
    return (
        array.reshape(seqs, pairs, count, span)
        .transpose(0, 2, 1, 3)
        .reshape(seqs, count, pairs * span)
    )


def masked_scores(query_heads, key_heads, query_place, query_group, key_place, key_group):
    scores = (
        jnp.einsum("qhd,khd->hqk", query_heads, key_heads, preferred_element_type=jnp.float32)
        * SCALE
    )
    allowed = (query_group[:, None] == key_group[None, :]) & (
        key_place[None, :] <= query_place[:, None]
    )
    return jnp.where(allowed[None], scores, NEGATIVE)


def attend_forward(
    queries, keys_all, values_all, query_places, query_groups, key_places, key_groups, pairs
):
    seqs, rows, width = queries.shape
    length = keys_all.shape[1]
    span = width // pairs
    tile = min(TILE, rows)

    def one_item(item):
        query_part, key_part, value_part, index = item
        which = index // pairs
        query_place = lax.dynamic_index_in_dim(query_places, which, 0, keepdims=False)
        query_group = lax.dynamic_index_in_dim(query_groups, which, 0, keepdims=False)
        key_place = lax.dynamic_index_in_dim(key_places, which, 0, keepdims=False)
        key_group = lax.dynamic_index_in_dim(key_groups, which, 0, keepdims=False)
        key_heads = key_part.reshape(length, 2, span // 2)
        value_heads = value_part.reshape(length, 2, span // 2)
        results, tops, totals = ([], [], [])
        query_heads = query_part.reshape(tile, 2, span // 2)
        scores = masked_scores(
            query_heads, key_heads, query_place, query_group, key_place, key_group
        )
        top = jnp.max(scores, axis=-1)
        raised = jnp.exp(scores - top[..., None])
        total = jnp.sum(raised, axis=-1)
        chance = (raised / total[..., None]).astype(jnp.bfloat16)
        mixed = jnp.einsum("hqk,khd->qhd", chance, value_heads, preferred_element_type=jnp.float32)
        results.append(mixed.reshape(tile, span).astype(jnp.bfloat16))
        tops.append(top)
        totals.append(total)
        return (
            jnp.concatenate(results, axis=0),
            jnp.concatenate(tops, axis=1),
            jnp.concatenate(totals, axis=1),
        )

    items = (
        split_pairs(queries, pairs),
        split_pairs(keys_all, pairs),
        split_pairs(values_all, pairs),
        jnp.arange(seqs * pairs, dtype=jnp.int32),
    )
    mixed, tops, totals = lax.map(one_item, items)
    return (join_pairs(mixed, seqs), tops, totals)


def attend_backward(
    queries,
    keys_all,
    values_all,
    attended_slope,
    tops,
    totals,
    query_places,
    query_groups,
    key_places,
    key_groups,
    pairs,
):
    seqs, rows, width = queries.shape
    length = keys_all.shape[1]
    span = width // pairs
    tile = min(TILE, rows)

    def one_item(item):
        query_part, key_part, value_part, slope_part, top, total, index = item
        which = index // pairs
        query_place = lax.dynamic_index_in_dim(query_places, which, 0, keepdims=False)
        query_group = lax.dynamic_index_in_dim(query_groups, which, 0, keepdims=False)
        key_place = lax.dynamic_index_in_dim(key_places, which, 0, keepdims=False)
        key_group = lax.dynamic_index_in_dim(key_groups, which, 0, keepdims=False)
        key_heads = key_part.reshape(length, 2, span // 2)
        value_heads = value_part.reshape(length, 2, span // 2)
        key_total = jnp.zeros((length, 2, span // 2), jnp.float32)
        value_total = jnp.zeros((length, 2, span // 2), jnp.float32)
        query_heads = query_part.reshape(tile, 2, span // 2)
        slope_heads = slope_part.reshape(tile, 2, span // 2)
        scores = masked_scores(
            query_heads, key_heads, query_place, query_group, key_place, key_group
        )
        chance = jnp.exp(scores - top[:, 0:tile, None]) / total[:, 0:tile, None]
        chance_low = chance.astype(jnp.bfloat16)
        value_total = value_total + jnp.einsum(
            "hqk,qhd->khd", chance_low, slope_heads, preferred_element_type=jnp.float32
        )
        pulled = jnp.einsum(
            "qhd,khd->hqk", slope_heads, value_heads, preferred_element_type=jnp.float32
        )
        score_slope = (chance * (pulled - jnp.sum(chance * pulled, axis=-1, keepdims=True))).astype(
            jnp.bfloat16
        )
        query_step = (
            jnp.einsum("hqk,khd->qhd", score_slope, key_heads, preferred_element_type=jnp.float32)
            * SCALE
        )
        query_results = [query_step.reshape(tile, span).astype(jnp.bfloat16)]
        key_total = (
            key_total
            + jnp.einsum(
                "hqk,qhd->khd", score_slope, query_heads, preferred_element_type=jnp.float32
            )
            * SCALE
        )
        return (
            jnp.concatenate(query_results, axis=0),
            key_total.reshape(length, span),
            value_total.reshape(length, span),
        )

    items = (
        split_pairs(queries, pairs),
        split_pairs(keys_all, pairs),
        split_pairs(values_all, pairs),
        split_pairs(attended_slope, pairs),
        tops,
        totals,
        jnp.arange(seqs * pairs, dtype=jnp.int32),
    )
    query_slope, key_part, value_part = lax.map(one_item, items)
    return (join_pairs(query_slope, seqs), join_pairs(key_part, seqs), join_pairs(value_part, seqs))


def on_device(
    layer_input,
    cotangent,
    segments,
    slot_order,
    first_gain,
    first_shift,
    project_weight,
    project_bias,
    output_weight,
    output_bias,
    second_gain,
    second_shift,
    expand_weight,
    expand_bias,
    shrink_weight,
    shrink_bias,
):
    seqs, rows, model_width = layer_input.shape
    count = seqs * rows
    half = rows // 2
    length = rows * lax.axis_size("ctx")
    begin = lax.axis_index("ctx") * rows
    local_width = project_weight.shape[2]
    pairs = local_width // (2 * HEAD_DIM)
    (
        gain_one,
        shift_one,
        project_full,
        output_full,
        out_bias,
        gain_two,
        shift_two,
        expand_full,
        shrink_full,
        shrink_add,
    ) = (
        lax.all_gather(first_gain, ("fsdp", "ctx"), axis=0, tiled=True),
        lax.all_gather(first_shift, ("fsdp", "ctx"), axis=0, tiled=True),
        lax.all_gather(project_weight, ("fsdp", "ctx"), axis=0, tiled=True),
        lax.all_gather(output_weight, ("fsdp", "ctx"), axis=1, tiled=True),
        lax.all_gather(output_bias, ("fsdp", "ctx"), axis=0, tiled=True),
        lax.all_gather(second_gain, ("fsdp", "ctx"), axis=0, tiled=True),
        lax.all_gather(second_shift, ("fsdp", "ctx"), axis=0, tiled=True),
        lax.all_gather(expand_weight, ("fsdp", "ctx"), axis=0, tiled=True),
        lax.all_gather(shrink_weight, ("fsdp", "ctx"), axis=1, tiled=True),
        lax.all_gather(shrink_bias, ("fsdp", "ctx"), axis=0, tiled=True),
    )
    offsets = jnp.arange(half, dtype=jnp.int32)
    key_places = (slot_order[:, :, None] * half + offsets[None, None, :]).reshape(seqs, length)
    query_places = lax.dynamic_slice_in_dim(key_places, begin, rows, 1)
    query_groups = lax.dynamic_slice_in_dim(segments, begin, rows, 1)
    inputs = layer_input.reshape(count, model_width).astype(jnp.float32)
    unit_one, inverse_one = normalize_parts(inputs)
    normed_one = (unit_one * gain_one.astype(jnp.float32) + shift_one.astype(jnp.float32)).astype(
        jnp.bfloat16
    )
    project_flat = project_full.reshape(model_width, 3 * local_width)
    mixed = jnp.dot(normed_one, project_flat, preferred_element_type=jnp.float32).reshape(
        count, 3, local_width
    )
    bias_pair = project_bias.astype(jnp.float32)
    queries = (mixed[:, 0] + bias_pair[0]).astype(jnp.bfloat16).reshape(seqs, rows, local_width)
    keys = mixed[:, 1].astype(jnp.bfloat16).reshape(seqs, rows, local_width)
    values = (mixed[:, 2] + bias_pair[1]).astype(jnp.bfloat16).reshape(seqs, rows, local_width)
    keys_all, values_all = (
        lax.all_gather(keys, "ctx", axis=1, tiled=True),
        lax.all_gather(values, "ctx", axis=1, tiled=True),
    )
    attended, tops, totals = attend_forward(
        queries, keys_all, values_all, query_places, query_groups, key_places, segments, pairs
    )
    attended_flat = attended.reshape(count, local_width)
    branch = lax.psum(jnp.dot(attended_flat, output_full, preferred_element_type=jnp.float32), "tp")
    middle = inputs + branch + out_bias.astype(jnp.float32)
    unit_two, inverse_two = normalize_parts(middle)
    normed_two = (unit_two * gain_two.astype(jnp.float32) + shift_two.astype(jnp.float32)).astype(
        jnp.bfloat16
    )
    before = jnp.dot(
        normed_two, expand_full, preferred_element_type=jnp.float32
    ) + expand_bias.astype(jnp.float32)
    active_value, gelu_pull = jax.vjp(partial(jax.nn.gelu, approximate=True), before)
    active = active_value.astype(jnp.bfloat16)
    feed = lax.psum(
        jnp.dot(active, shrink_full, preferred_element_type=jnp.float32).astype(jnp.bfloat16), "tp"
    ).astype(jnp.float32)
    layer_output = (
        (middle + feed + shrink_add.astype(jnp.float32))
        .astype(jnp.bfloat16)
        .reshape(seqs, rows, model_width)
    )
    gain_back, project_again, output_back, gain_two_back, expand_back, shrink_back = (
        lax.all_gather(first_gain, ("fsdp", "ctx"), axis=0, tiled=True),
        lax.all_gather(project_weight, ("fsdp", "ctx"), axis=0, tiled=True),
        lax.all_gather(output_weight, ("fsdp", "ctx"), axis=1, tiled=True),
        lax.all_gather(second_gain, ("fsdp", "ctx"), axis=0, tiled=True),
        lax.all_gather(expand_weight, ("fsdp", "ctx"), axis=0, tiled=True),
        lax.all_gather(shrink_weight, ("fsdp", "ctx"), axis=1, tiled=True),
    )
    project_back = project_again.reshape(model_width, 3 * local_width)
    slope = cotangent.reshape(count, model_width).astype(jnp.float32)
    shrink_bias_delta = jnp.sum(slope, axis=0)
    slope_low = slope.astype(jnp.bfloat16)
    shrink_weight_delta = contract_rows(active, slope_low)
    active_slope = times_transpose(slope_low, shrink_back)
    before_slope = gelu_pull(active_slope)[0].astype(jnp.bfloat16)
    expand_bias_delta = jnp.sum(before_slope.astype(jnp.float32), axis=0)
    expand_weight_delta = contract_rows(normed_two, before_slope)
    normed_two_slope = lax.psum(
        times_transpose(before_slope, expand_back).astype(jnp.bfloat16), "tp"
    ).astype(jnp.float32)
    back_two, gain_two_delta, shift_two_delta = norm_backward(
        normed_two_slope, unit_two, inverse_two, gain_two_back.astype(jnp.float32)
    )
    middle_slope = slope + back_two
    output_bias_delta = jnp.sum(middle_slope, axis=0)
    middle_low = middle_slope.astype(jnp.bfloat16)
    output_weight_delta = contract_rows(attended_flat, middle_low)
    attended_slope = (
        times_transpose(middle_low, output_back)
        .astype(jnp.bfloat16)
        .reshape(seqs, rows, local_width)
    )
    query_slope, key_part, value_part = attend_backward(
        queries,
        keys_all,
        values_all,
        attended_slope,
        tops,
        totals,
        query_places,
        query_groups,
        key_places,
        segments,
        pairs,
    )
    key_slope, value_slope = (
        lax.psum_scatter(
            key_part.astype(jnp.bfloat16), "ctx", scatter_dimension=1, tiled=True
        ).astype(jnp.float32),
        lax.psum_scatter(
            value_part.astype(jnp.bfloat16), "ctx", scatter_dimension=1, tiled=True
        ).astype(jnp.float32),
    )
    key_low = key_slope.astype(jnp.bfloat16)
    value_low = value_slope.astype(jnp.bfloat16)
    project_slope = jnp.stack([query_slope, key_low, value_low], axis=2).reshape(
        count, 3 * local_width
    )
    project_weight_delta = contract_rows(normed_one, project_slope).reshape(
        model_width, 3, local_width
    )
    project_bias_delta = jnp.stack(
        [
            jnp.sum(query_slope.reshape(count, local_width).astype(jnp.float32), axis=0),
            jnp.sum(value_low.reshape(count, local_width).astype(jnp.float32), axis=0),
        ]
    )
    normed_one_slope = lax.psum(
        times_transpose(project_slope, project_back).astype(jnp.bfloat16), "tp"
    ).astype(jnp.float32)
    back_one, gain_one_delta, shift_one_delta = norm_backward(
        normed_one_slope, unit_one, inverse_one, gain_back.astype(jnp.float32)
    )
    input_delta = (middle_slope + back_one).reshape(seqs, rows, model_width)
    (
        part_gain_one,
        part_shift_one,
        part_project,
        part_output,
        part_out_bias,
        part_gain_two,
        part_shift_two,
        part_expand,
        part_shrink,
        part_shrink_bias,
    ) = (
        lax.psum_scatter(
            gain_one_delta.astype(jnp.bfloat16), "fsdp", scatter_dimension=0, tiled=True
        ).astype(jnp.float32),
        lax.psum_scatter(
            shift_one_delta.astype(jnp.bfloat16), "fsdp", scatter_dimension=0, tiled=True
        ).astype(jnp.float32),
        lax.psum_scatter(
            project_weight_delta.astype(jnp.bfloat16), "fsdp", scatter_dimension=0, tiled=True
        ).astype(jnp.float32),
        lax.psum_scatter(
            output_weight_delta.astype(jnp.bfloat16), "fsdp", scatter_dimension=1, tiled=True
        ).astype(jnp.float32),
        lax.psum_scatter(
            output_bias_delta.astype(jnp.bfloat16), "fsdp", scatter_dimension=0, tiled=True
        ).astype(jnp.float32),
        lax.psum_scatter(
            gain_two_delta.astype(jnp.bfloat16), "fsdp", scatter_dimension=0, tiled=True
        ).astype(jnp.float32),
        lax.psum_scatter(
            shift_two_delta.astype(jnp.bfloat16), "fsdp", scatter_dimension=0, tiled=True
        ).astype(jnp.float32),
        lax.psum_scatter(
            expand_weight_delta.astype(jnp.bfloat16), "fsdp", scatter_dimension=0, tiled=True
        ).astype(jnp.float32),
        lax.psum_scatter(
            shrink_weight_delta.astype(jnp.bfloat16), "fsdp", scatter_dimension=1, tiled=True
        ).astype(jnp.float32),
        lax.psum_scatter(
            shrink_bias_delta.astype(jnp.bfloat16), "fsdp", scatter_dimension=0, tiled=True
        ).astype(jnp.float32),
    )
    shares = (
        lax.psum_scatter(
            part_gain_one.astype(jnp.bfloat16), "ctx", scatter_dimension=0, tiled=True
        ).astype(jnp.float32),
        lax.psum_scatter(
            part_shift_one.astype(jnp.bfloat16), "ctx", scatter_dimension=0, tiled=True
        ).astype(jnp.float32),
        lax.psum_scatter(
            part_project.astype(jnp.bfloat16), "ctx", scatter_dimension=0, tiled=True
        ).astype(jnp.float32),
        lax.psum_scatter(
            part_output.astype(jnp.bfloat16), "ctx", scatter_dimension=1, tiled=True
        ).astype(jnp.float32),
        lax.psum_scatter(
            part_out_bias.astype(jnp.bfloat16), "ctx", scatter_dimension=0, tiled=True
        ).astype(jnp.float32),
        lax.psum_scatter(
            part_gain_two.astype(jnp.bfloat16), "ctx", scatter_dimension=0, tiled=True
        ).astype(jnp.float32),
        lax.psum_scatter(
            part_shift_two.astype(jnp.bfloat16), "ctx", scatter_dimension=0, tiled=True
        ).astype(jnp.float32),
        lax.psum_scatter(
            part_expand.astype(jnp.bfloat16), "ctx", scatter_dimension=0, tiled=True
        ).astype(jnp.float32),
        lax.psum_scatter(
            part_shrink.astype(jnp.bfloat16), "ctx", scatter_dimension=1, tiled=True
        ).astype(jnp.float32),
        lax.psum_scatter(
            part_shrink_bias.astype(jnp.bfloat16), "ctx", scatter_dimension=0, tiled=True
        ).astype(jnp.float32),
    )
    bias_sums = lax.psum((project_bias_delta, expand_bias_delta), ("fsdp", "ctx"))
    return (
        layer_output,
        input_delta,
        shares[0],
        shares[1],
        shares[2],
        bias_sums[0],
        shares[3],
        shares[4],
        shares[5],
        shares[6],
        shares[7],
        bias_sums[1],
        shares[8],
        shares[9],
    )


def solution(mesh):
    return jax.shard_map(
        on_device,
        mesh=mesh,
        in_specs=(
            P("fsdp", "ctx", None),
            P("fsdp", "ctx", None),
            P("fsdp", None),
            P("fsdp", None),
            P(("fsdp", "ctx")),
            P(("fsdp", "ctx")),
            P(("fsdp", "ctx"), None, "tp"),
            P(None, "tp"),
            P("tp", ("fsdp", "ctx")),
            P(("fsdp", "ctx")),
            P(("fsdp", "ctx")),
            P(("fsdp", "ctx")),
            P(("fsdp", "ctx"), "tp"),
            P("tp"),
            P("tp", ("fsdp", "ctx")),
            P(("fsdp", "ctx")),
        ),
        out_specs=(
            P("fsdp", "ctx", None),
            P("fsdp", "ctx", None),
            P(("fsdp", "ctx")),
            P(("fsdp", "ctx")),
            P(("fsdp", "ctx"), None, "tp"),
            P(None, "tp"),
            P("tp", ("fsdp", "ctx")),
            P(("fsdp", "ctx")),
            P(("fsdp", "ctx")),
            P(("fsdp", "ctx")),
            P(("fsdp", "ctx"), "tp"),
            P("tp"),
            P("tp", ("fsdp", "ctx")),
            P(("fsdp", "ctx")),
        ),
        check_vma=False,
    )
```

profile of v0, /device:TPU:0, one launch (start us, length us, event | category | flops | bytes accessed | tf_op | source)
XLA Modules:
  0.0 796.2 jit_solution(2698186642065750225)
XLA Ops:
  14.9 63.5 %all-reduce.19 = (bf16[768]{0:T(1024)(128)(2,1)S(1)}, bf16[768]{0:T(1024)(128)(2,1)S(1)}, bf16[768]{0:T(1024)(128)(2,1)}, bf16[768]{0:T(1024)(128)(2,1)}, bf16[768]{0:T(1024)(128)(2,1)}, /*index=5*/bf16[768]{0:T(1024)(128)(2,1)}) all-reduce(bf16[768]{0:T(1024)(128)(2,1)S(1)} %dynamic-update-slice, ...), channel_id=1, replica_groups=mesh['fsdp'=4,'ctx'=4,'tp'=2] {'fsdp','ctx'}, use_global_device_ids=true, to_apply=%add.1 | all-reduce | flops 4608 | bytes 18432
  80.4 1.5 fusion.37
  82.0 2.7 copy.43
  88.4 2.0 slice.64
  90.7 21.1 %all_gather.47 = bf16[384,768]{0,1:T(8,128)(2,1)} all-gather(bf16[384,48]{0,1:T(8,128)(2,1)S(1)} %copy-done.30), channel_id=1, replica_groups=mesh['fsdp'=4,'ctx'=4,'tp'=2] {'fsdp','ctx'}, dimensions={1}, use_global_device_ids=true | all-gather | bytes 626688 | tf_op jit(solution)/shard_map/all_gather | solution.py:240
  112.7 1.5 fusion.70
  115.9 14.8 %all-gather.15.cloned.1.call-done = bf16[2048,1,384]{0,2,1:T(8,128)(2,1)} async-done(((bf16[512,1,384]{0,2,1:T(8,128)(2,1)}), bf16[2048,1,384]{0,2,1:T(8,128)(2,1)}) %all-gather.15.cloned.1.call-update) | async-done | bytes 1572880 | tf_op jit(solution)/shard_map/all_gather | solution.py:266
  130.7 1.5 fusion.69
  132.3 1.6 copy.45
  133.8 1.7 copy.47
  135.6 31.4 %while.32 = (s32[]{:T(128)}, bf16[3,512,128]{1,2,0:T(8,128)(2,1)S(1)}, f32[3,2,512]{2,1,0:T(2,128)}, f32[3,2,512]{2,1,0:T(2,128)}, bf16[3,2048,128]{1,2,0:T(8,12...) while((s32[]{:T(128)}, ...), condition=%wide.region_5.6_spmd.clone, body=%wide.region_2.5_spmd.clone.sunk | while | flops 565248000 | bytes 33407152 | solution.py:120
  138.3 2.0 fusion.119
  140.3 2.5 fusion.120
  142.8 2.6 fusion.121
  148.8 2.0 fusion.119
  150.8 2.5 fusion.120
  153.3 2.6 fusion.121
  159.3 2.0 fusion.119
  161.3 2.5 fusion.120
  163.8 2.6 fusion.121
  167.1 3.2 fusion.72
  176.8 45.2 %all-reduce.27.cloned.1.call-done = f32[512,768]{1,0:T(8,128)} async-done(((f32[512,768]{1,0:T(8,128)}), f32[512,768]{1,0:T(8,128)}) %all-reduce.27.cloned.1.call-update) | async-done | bytes 1572880 | tf_op jit(solution)/shard_map/psum | solution.py:273
  222.0 1.9 fusion.67
  225.5 41.0 %all-gather.11.cloned.1.call-done = bf16[768,1536]{1,0:T(8,128)(2,1)} async-done(((bf16[48,1536]{1,0:T(8,128)(2,1)}), bf16[768,1536]{1,0:T(8,128)(2,1)}) %all-gather.11.cloned.1.call-update) | async-done | bytes 2359312 | tf_op jit(solution)/shard_map/all_gather | solution.py:244
  266.5 4.9 convolution_add_fusion
  271.3 38.3 %all-gather.13.cloned.1.call-done = bf16[1536,768]{0,1:T(8,128)(2,1)} async-done(((bf16[1536,48]{0,1:T(8,128)(2,1)}), bf16[1536,768]{0,1:T(8,128)(2,1)}) %all-gather.13.cloned.1.call-update) | async-done | bytes 2359312 | tf_op jit(solution)/shard_map/all_gather | solution.py:245
  309.7 6.6 convert_reduce_fusion
  317.4 2.3 convolution_convert_fusion.3
  319.8 33.2 %all-reduce.29.cloned.1.call-done = bf16[512,768]{1,0:T(8,128)(2,1)} async-done(((bf16[512,768]{1,0:T(8,128)(2,1)}), bf16[512,768]{1,0:T(8,128)(2,1)}) %all-reduce.29.cloned.1.call-update) | async-done | bytes 786448 | tf_op jit(solution)/shard_map/psum | solution.py:309
  353.0 2.6 fusion.42
  355.7 2.0 fusion.65
  361.4 79.7 %while.33 = (s32[]{:T(128)}, bf16[3,512,128]{1,2,0:T(8,128)(2,1)}, bf16[3,2048,128]{1,2,0:T(8,128)(2,1)}, bf16[3,2048,128]{1,2,0:T(8,128)(2,1)}, bf16[3,2048,128...) while((s32[]{:T(128)}, bf16[3,512,128]{1,2,0:T(8,128)(2,1)}, ...), condition=%wide.region_15.16_spmd.clone, body=%wide.region_13.15_spmd.clone.sunk | while | flops 1366950912 | bytes 122663424 | solution.py:196
  366.6 5.9 multiply_reduce_fusion.3
  372.5 6.6 multiply_convert_fusion.5
  379.1 4.3 fusion.134
  393.3 5.9 multiply_reduce_fusion.3
  399.2 6.6 multiply_convert_fusion.5
  405.7 4.2 fusion.134
  419.8 5.9 multiply_reduce_fusion.3
  425.7 6.6 multiply_convert_fusion.5
  432.2 4.2 fusion.134
  442.3 5.0 convolution_convert_fusion
  448.8 3.0 convolution_convert_fusion.1
  452.2 5.5 convolution_convert_fusion.4
  457.7 11.7 %reduce-scatter.11.cloned.1.call-done = bf16[1,512,384]{1,2,0:T(8,128)(2,1)} async-done(((bf16[1,2048,384]{1,2,0:T(8,128)(2,1)}), bf16[1,512,384]{1,2,0:T(8,128)(2,1)}) %reduce-scatter.11.cloned.1.call-update) | async-done | bytes 393232 | tf_op jit(solution)/shard_map/reduce_scatter | solution.py:338
  469.3 30.4 %reduce-scatter.13.cloned.1.call-done = bf16[1,512,384]{1,2,0:T(8,128)(2,1)} async-done(((bf16[1,2048,384]{1,2,0:T(8,128)(2,1)}), bf16[1,512,384]{1,2,0:T(8,128)(2,1)}) %reduce-scatter.13.cloned.1.call-update) | async-done | bytes 393232 | tf_op jit(solution)/shard_map/reduce_scatter | solution.py:341
  501.2 2.1 convolution_convert_fusion.5
  504.6 3.7 convolution_convert_fusion.2
  508.5 41.4 %reduce-scatter.27.cloned.1.call-done = bf16[1536,192]{0,1:T(8,128)(2,1)} async-done(((bf16[1536,768]{0,1:T(8,128)(2,1)}), bf16[1536,192]{0,1:T(8,128)(2,1)}) %reduce-scatter.27.cloned.1.call-update) | async-done | bytes 589840 | tf_op jit(solution)/shard_map/reduce_scatter | solution.py:402
  551.7 1.9 reduce_sum.198
  557.0 14.2 %reduce-scatter.21.cloned.1.call-done = bf16[384,48]{0,1:T(8,128)(2,1)} async-done(((bf16[384,192]{0,1:T(8,128)(2,1)}), bf16[384,48]{0,1:T(8,128)(2,1)}) %reduce-scatter.21.cloned.1.call-update) | async-done | bytes 36880 | tf_op jit(solution)/shard_map/reduce_scatter | solution.py:419
  572.6 48.6 %reduce-scatter.23.cloned.1.call-done = bf16[192,1536]{1,0:T(8,128)(2,1)} async-done(((bf16[768,1536]{1,0:T(8,128)(2,1)}), bf16[192,1536]{1,0:T(8,128)(2,1)}) %reduce-scatter.23.cloned.1.call-update) | async-done | bytes 589840 | tf_op jit(solution)/shard_map/reduce_scatter | solution.py:399
  622.2 59.5 %all-reduce.18 = (f32[2,384]{1,0:T(2,128)}, f32[1536]{0:T(1024)}) all-reduce(f32[2,384]{1,0:T(2,128)S(1)} %pad_maximum_fusion.3, f32[1536]{0:T(1024)} %get-tuple-element.444), channel_id=1, replica_groups=mesh['fsdp'=4,'ctx'=4,'tp'=2] {'fsdp','ctx'}, use_global_device_ids=true, to_apply=%region_31.32 | all-reduce | flops 2304 | bytes 18432 | tf_op jit(solution)/shard_map/psum | solution.py:441
  683.0 2.0 fusion.44
  685.0 17.3 %all-reduce.21 = (bf16[768]{0:T(1024)(128)(2,1)S(1)}, bf16[768]{0:T(1024)(128)(2,1)S(1)}, bf16[768]{0:T(1024)(128)(2,1)S(1)}, bf16[768]{0:T(1024)(128)(2,1)S(1)}...) all-reduce(bf16[768]{0:T(1024)(128)(2,1)S(1)} %get-tuple-element.34, ...), channel_id=5, replica_groups=mesh['fsdp'=4,'ctx'=4,'tp'=2] {'fsdp'}, use_global_device_ids=true, to_apply=%region_22.23.clone | all-reduce | flops 4608 | bytes 18432
  702.7 6.0 all-reduce.20
  711.7 4.4 reduce-scatter.15.cloned.1.call-done
  718.6 1.7 fusion.36
  720.3 19.2 %reduce-scatter.29.cloned.1.call-done = bf16[1536,48]{0,1:T(8,128)(2,1)} async-done(((bf16[1536,192]{0,1:T(8,128)(2,1)}), bf16[1536,48]{0,1:T(8,128)(2,1)}) %reduce-scatter.29.cloned.1.call-update) | async-done | bytes 147472 | tf_op jit(solution)/shard_map/reduce_scatter | solution.py:434
  739.5 1.6 convert_element_type.341
  741.2 22.8 %reduce-scatter.25.cloned.1.call-done = bf16[48,1536]{1,0:T(8,128)(2,1)} async-done(((bf16[192,1536]{1,0:T(8,128)(2,1)}), bf16[48,1536]{1,0:T(8,128)(2,1)}) %reduce-scatter.25.cloned.1.call-update) | async-done | bytes 147472 | tf_op jit(solution)/shard_map/reduce_scatter | solution.py:431
  764.0 1.6 convert_element_type.338
  765.6 21.9 %reduce-scatter.17.cloned.1.call-done = bf16[48,3,384]{2,0,1:T(8,128)(2,1)} async-done(((bf16[192,3,384]{2,0,1:T(8,128)(2,1)}), bf16[48,3,384]{2,0,1:T(8,128)(2,1)}) %reduce-scatter.17.cloned.1.call-update) | async-done | bytes 110608 | tf_op jit(solution)/shard_map/reduce_scatter | solution.py:416
  787.5 1.6 convert_element_type.327
  (311 shorter events, 87.0 us)
Async XLA Ops:
  7.2 74.8 %all-gather.7.cloned.1.call-start = ((), (), s32[]{:S(2)}) async-start(), calls=%async_computation.10 | async-start | bytes 1880064 | tf_op jit(solution)/shard_map/all_gather | solution.py:239
  7.9 104.7 %all-gather.9.cloned.1.call-start = ((), (), s32[]{:S(2)}) async-start(), calls=%async_computation.11 | async-start | bytes 1966080 | tf_op jit(solution)/shard_map/all_gather | solution.py:267
  78.4 6.3 copy-start.40
  79.1 5.6 copy-start.31
  80.4 4.3 copy-start.35
  81.9 2.8 copy-start.38
  81.9 2.8 copy-start.8
  86.0 4.4 copy-start.44
  86.1 4.6 copy-start.24
  86.1 4.6 copy-start.30
  88.3 42.3 %all-gather.15.cloned.1.call-start = ((), (), s32[]{:S(2)}) async-start(), calls=%async_computation.26 | async-start | bytes 1966080 | tf_op jit(solution)/shard_map/all_gather | solution.py:266
  88.4 23.4 %slice-start = ((f32[512,3,384]{0,2,1:T(8,128)}), f32[512,1,384]{0,2,1:T(8,128)S(1)}, s32[]{:S(2)}) async-start(f32[512,3,384]{0,2,1:T(8,128)} %copy-done.19), calls=%async_computation.28 | async-start | bytes 1572864 | tf_op jit(solution)/shard_map/slice | solution.py:262
  90.4 131.6 %all-reduce.27.cloned.1.call-start = ((), (), s32[]{:S(2)}) async-start(), calls=%async_computation.12 | async-start | bytes 3145728 | tf_op jit(solution)/shard_map/psum | solution.py:273
  90.5 22.1 %copy-start.26 = (s32[8]{0:T(128)}, s32[8]{0:T(128)S(1)}, u32[]{:S(2)}) copy-start(s32[8]{0:T(128)S(1)} %multiply_bitcast_fusion) | copy-start | bytes 100
  167.0 3.3 copy-start.3
  170.3 96.2 %all-gather.11.cloned.1.call-start = ((), (), s32[]{:S(2)}) async-start(), calls=%async_computation.13 | async-start | bytes 2506752 | tf_op jit(solution)/shard_map/all_gather | solution.py:244
  170.9 138.8 %all-gather.13.cloned.1.call-start = ((), (), s32[]{:S(2)}) async-start(), calls=%async_computation.14 | async-start | bytes 2506752 | tf_op jit(solution)/shard_map/all_gather | solution.py:245
  171.5 181.5 %all-reduce.29.cloned.1.call-start = ((), (), s32[]{:S(2)}) async-start(), calls=%async_computation.15 | async-start | bytes 1572864 | tf_op jit(solution)/shard_map/psum | solution.py:309
  223.9 131.8 %copy-start.1 = (f32[512,768]{1,0:T(8,128)}, f32[512,768]{1,0:T(8,128)S(1)}, u32[]{:S(2)}) copy-start(f32[512,768]{1,0:T(8,128)S(1)} %get-tuple-element.425) | copy-start | bytes 4718596
  309.7 7.7 copy-start.43
  319.7 127.7 %reduce-scatter.19.cloned.1.call-start = ((), (), s32[]{:S(2)}) async-start(), calls=%async_computation.20 | async-start | bytes 737280 | tf_op jit(solution)/shard_map/reduce_scatter | solution.py:387
  353.0 2.7 copy-start.12
  353.0 2.7 copy-start.17
  355.7 2.0 copy-start.15
  358.9 2.5 copy-start.27
  360.4 108.9 %reduce-scatter.11.cloned.1.call-start = ((), (), s32[]{:S(2)}) async-start(), calls=%async_computation.16 | async-start | bytes 1966080 | tf_op jit(solution)/shard_map/reduce_scatter | solution.py:338
  361.4 3.9 copy-start.20
  361.4 5.2 copy-start.4
  366.6 5.9 copy-start
  385.7 2.4 copy-start.5
  385.7 2.4 copy-start.21
  385.7 2.4 copy-start.28
  388.1 3.9 copy-start.20
  388.1 5.2 copy-start.4
  393.3 5.9 copy-start
  412.2 2.4 copy-start.5
  412.2 2.4 copy-start.21
  412.2 2.4 copy-start.28
  414.6 3.9 copy-start.20
  414.6 5.2 copy-start.4
  419.8 5.9 copy-start
  438.8 2.4 copy-start.5
  438.8 2.4 copy-start.21
  438.8 2.4 copy-start.28
  441.2 58.6 %reduce-scatter.13.cloned.1.call-start = ((), (), s32[]{:S(2)}) async-start(), calls=%async_computation.17 | async-start | bytes 1966080 | tf_op jit(solution)/shard_map/reduce_scatter | solution.py:341
  441.8 108.0 %reduce-scatter.27.cloned.1.call-start = ((), (), s32[]{:S(2)}) async-start(), calls=%async_computation.24 | async-start | bytes 2949120 | tf_op jit(solution)/shard_map/reduce_scatter | solution.py:402
  442.3 5.7 copy-start.47
  447.3 123.9 %reduce-scatter.21.cloned.1.call-start = ((), (), s32[]{:S(2)}) async-start(), calls=%async_computation.21 | async-start | bytes 184320 | tf_op jit(solution)/shard_map/reduce_scatter | solution.py:419
  447.9 173.3 %reduce-scatter.23.cloned.1.call-start = ((), (), s32[]{:S(2)}) async-start(), calls=%async_computation.22 | async-start | bytes 2949120 | tf_op jit(solution)/shard_map/reduce_scatter | solution.py:399
  451.9 229.7 %all-reduce.31.cloned.1.call-start = ((), (), s32[]{:S(2)}) async-start(), calls=%async_computation.27 | async-start | bytes 3145728 | tf_op jit(solution)/shard_map/psum | solution.py:284
  457.7 43.5 %copy-start.11 = (bf16[768,3,384]{0,2,1:T(8,128)(2,1)S(1)}, bf16[768,3,384]{0,2,1:T(8,128)(2,1)}, u32[]{:S(2)}) copy-start(bf16[768,3,384]{0,2,1:T(8,128)(2,1)} %copy-done.10) | copy-start | bytes 5308420
  501.1 2.2 copy-start.36
  501.1 2.2 copy-start.39
  501.2 2.2 copy-start.41
  503.3 212.8 %reduce-scatter.15.cloned.1.call-start = ((), (), s32[]{:S(2)}) async-start(), calls=%async_computation.18 | async-start | bytes 2211840 | tf_op jit(solution)/shard_map/reduce_scatter | solution.py:384
  508.4 42.8 %copy-start.45 = (u32[32]{0:T(128)S(1)}, u32[32]{0:T(128)}, u32[]{:S(2)}) copy-start(u32[32]{0:T(128)} %constant.177) | copy-start | bytes 388
  508.4 47.9 %copy-start.13 = (bf16[512,768]{1,0:T(8,128)(2,1)S(1)}, bf16[512,768]{1,0:T(8,128)(2,1)}, u32[]{:S(2)}) copy-start(bf16[512,768]{1,0:T(8,128)(2,1)} %all-reduce.29.cloned.1.call-done) | copy-start | bytes 2359300
  508.4 231.1 %reduce-scatter.29.cloned.1.call-start = ((), (), s32[]{:S(2)}) async-start(), calls=%async_computation.25 | async-start | bytes 737280 | tf_op jit(solution)/shard_map/reduce_scatter | solution.py:434
  549.9 214.1 %reduce-scatter.25.cloned.1.call-start = ((), (), s32[]{:S(2)}) async-start(), calls=%async_computation.23 | async-start | bytes 737280 | tf_op jit(solution)/shard_map/reduce_scatter | solution.py:431
  555.7 65.6 %copy-start.23 = (bf16[1,512,384]{1,2,0:T(8,128)(2,1)S(1)}, bf16[1,512,384]{1,2,0:T(8,128)(2,1)}, u32[]{:S(2)}) copy-start(bf16[1,512,384]{1,2,0:T(8,128)(2,1)} %reduce-scatter.13.cloned.1.call-done) | copy-start | bytes 1179652
  621.3 166.2 %reduce-scatter.17.cloned.1.call-start = ((), (), s32[]{:S(2)}) async-start(), calls=%async_computation.19 | async-start | bytes 552960 | tf_op jit(solution)/shard_map/reduce_scatter | solution.py:416
  681.6 35.1 %copy-start.25 = (bf16[512,768]{1,0:T(8,128)(2,1)S(1)}, bf16[512,768]{1,0:T(8,128)(2,1)}, u32[]{:S(2)}) copy-start(bf16[512,768]{1,0:T(8,128)(2,1)} %get-tuple-element.420) | copy-start | bytes 2359300
  716.7 1.7 copy-start.7
  716.7 1.9 copy-start.14
  (15 other events, 19.6 us)
Sparse Core Ops, SparseCore 0:
  10.3 43.3 all-gather.6
  88.5 20.4 all-gather.8
  111.1 19.5 all-gather.14
  170.4 51.5 all-reduce.26
  224.1 42.3 all-gather.10
  268.6 41.0 all-gather.12
  319.9 33.0 all-reduce.28
  360.5 22.1 reduce-scatter.18
  441.3 27.9 reduce-scatter.10
  471.7 28.0 reduce-scatter.12
  502.1 47.7 reduce-scatter.26
  552.1 19.0 reduce-scatter.20
  573.5 47.6 reduce-scatter.22
  624.0 50.8 all-reduce.30
  677.1 38.9 reduce-scatter.14
  718.4 21.0 reduce-scatter.28
  741.9 22.0 reduce-scatter.24
  766.3 21.1 reduce-scatter.16
where the time goes:
time: 801 us; the launch traced here: 796 us
  waiting for transfers between devices  390 us (49%)
  blocking collectives  167 us (21%)
  matrix products  94.3 us (12%)
  other arithmetic  72.5 us (9%)
  local copies, waits for them, and re-layouts  52.9 us (7%)
  between operations  17.1 us (2%)
    unnamed x3, blocking collectives  86.8 us
    psum x1, blocking collectives, on_device(): lax.psum((project_bias_delta, expand_bias_delta), ('fsdp', 'ctx'))  59.5 us
    reduce_scatter x1, waiting for transfers between devices, on_device(): lax.psum_scatter(expand_weight_delta.astype(jnp.bfloat16), 'fsdp', scatte...  48.6 us
    psum x1, waiting for transfers between devices, on_device(): lax.psum(jnp.dot(attended_flat, output_full, preferred_element_type=jnp.f...  45.2 us
    reduce_scatter x1, waiting for transfers between devices, on_device(): lax.psum_scatter(shrink_weight_delta.astype(jnp.bfloat16), 'fsdp', scatte...  41.4 us
    all_gather x1, waiting for transfers between devices, on_device(): lax.all_gather(expand_weight, ('fsdp', 'ctx'), axis=0, tiled=True)  41 us
    all_gather x1, waiting for transfers between devices, on_device(): lax.all_gather(shrink_weight, ('fsdp', 'ctx'), axis=1, tiled=True)  38.3 us
    psum x1, waiting for transfers between devices, on_device(): lax.psum(times_transpose(before_slope, expand_back).astype(jnp.bfloat16),...  33.2 us
  transfers between devices with their start and end apart: 18, of which 14 were waited for; matrix products, arithmetic and copies ran while one was open for 19% of the time, Pallas kernels for 0%

commit v1 on v0

--- a/solution.py
+++ b/solution.py
@@ -3,6 +3,8 @@
 import jax
 import jax.numpy as jnp
 from jax import lax
+from jax.experimental import pallas as pl
+from jax.experimental.pallas import tpu as pltpu
 from jax.sharding import PartitionSpec as P
 
 HEAD_DIM = 64
@@ -12,6 +14,8 @@
 SCALE = 0.125
 NEGATIVE = -1000000000.0
 TILE = 512
+GELU_A = 0.7978845608028654
+GELU_B = 0.044715
 
 
 def contract_rows(left, right):
@@ -457,9 +461,1280 @@
     )
 
 
+MESH = pl.DeviceIdType.MESH
+VMEM_BYTES = 62 * 1024 * 1024
+
+
+def dot_nn(left, right):
+    return lax.dot_general(
+        left, right, (((1,), (0,)), ((), ())), preferred_element_type=jnp.float32
+    )
+
+
+def dot_nt(left, right):
+    return lax.dot_general(
+        left, right, (((1,), (1,)), ((), ())), preferred_element_type=jnp.float32
+    )
+
+
+def remote(source, target, send, receive, device):
+    return pltpu.make_async_remote_copy(
+        src_ref=source,
+        dst_ref=target,
+        send_sem=send,
+        recv_sem=receive,
+        device_id=device,
+        device_id_type=MESH,
+    )
+
+
+def aligned(index, size, unit=16):
+    return pl.ds(pl.multiple_of(index * size, unit), size)
+
+
+class Place:
+    def __init__(self, line):
+        self.line = line
+        self.f = lax.axis_index("fsdp")
+        self.c = lax.axis_index("ctx")
+        self.t = lax.axis_index("tp")
+        self.core_bit = lax.rem(self.c, 2)
+        self.row_bit = self.c // 2
+        self.core = self.c + 1 - 2 * self.core_bit
+        self.row = lax.rem(self.c + 2, 4)
+        self.core_device = (self.f, self.core, self.t)
+        self.row_device = (self.f, self.row, self.t)
+        self.tp_device = (self.f, self.c, 1 - self.t)
+
+    def line_device(self, f):
+        return (f, self.c, self.t)
+
+    def greet(self, tp, line):
+        barrier = pltpu.get_barrier_semaphore()
+        count = 2
+        pl.semaphore_signal(barrier, 1, device_id=self.core_device, device_id_type=MESH)
+        pl.semaphore_signal(barrier, 1, device_id=self.row_device, device_id_type=MESH)
+        if tp:
+            pl.semaphore_signal(barrier, 1, device_id=self.tp_device, device_id_type=MESH)
+            count += 1
+        if line:
+            for step in range(1, self.line):
+                pl.semaphore_signal(
+                    barrier,
+                    1,
+                    device_id=self.line_device(lax.rem(self.f + step, self.line)),
+                    device_id_type=MESH,
+                )
+            count += self.line - 1
+        pl.semaphore_wait(barrier, count)
+
+
+class Scatter:
+    def __init__(self, place, group, shard, sems, core=None, row=None, line=None):
+        self.place, self.group, self.shard = place, group, shard
+        self.core_send, self.core_recv, self.row_send, self.row_recv, self.line_send, self.line_recv = sems
+        self.core, self.row, self.line = core, row, line
+
+    def core_copies(self):
+        full, landed, _ = self.core
+        at = self.place
+        copies = []
+        for f in range(at.line):
+            for y in range(2):
+                index = f * 2 + y
+                copies.append(
+                    remote(
+                        full.at[aligned(f * 4 + 2 * y + 1 - at.core_bit, self.shard), :],
+                        landed.at[pl.ds(index * self.shard, self.shard), :],
+                        self.core_send.at[self.group, index],
+                        self.core_recv.at[self.group, index],
+                        at.core_device,
+                    )
+                )
+        return copies
+
+    def row_copies(self):
+        summed, landed, _ = self.row
+        at = self.place
+        return [
+            remote(
+                summed.at[aligned(f * 2 + 1 - at.row_bit, self.shard), :],
+                landed.at[pl.ds(f * self.shard, self.shard), :],
+                self.row_send.at[self.group, f],
+                self.row_recv.at[self.group, f],
+                at.row_device,
+            )
+            for f in range(at.line)
+        ]
+
+    def line_copies(self):
+        summed, landed, _ = self.line
+        at = self.place
+        copies = []
+        for step in range(1, at.line):
+            target = lax.rem(at.f + step, at.line)
+            copies.append(
+                remote(
+                    summed.at[aligned(target, self.shard), :],
+                    landed.at[pl.ds((step - 1) * self.shard, self.shard), :],
+                    self.line_send.at[self.group, step],
+                    self.line_recv.at[self.group, step],
+                    at.line_device(target),
+                )
+            )
+        return copies
+
+    def start(self, stage):
+        for copy in getattr(self, stage + "_copies")():
+            copy.start()
+
+    def core_finish(self):
+        full, landed, summed = self.core
+        at = self.place
+        for index, copy in enumerate(self.core_copies()):
+            copy.wait_recv()
+            f, y = index // 2, index % 2
+            own = full[aligned(f * 4 + 2 * y + at.core_bit, self.shard), :]
+            other = landed[index * self.shard : (index + 1) * self.shard, :]
+            summed[index * self.shard : (index + 1) * self.shard, :] = (
+                own.astype(jnp.float32) + other.astype(jnp.float32)
+            ).astype(summed.dtype)
+
+    def row_finish(self):
+        summed, landed, result = self.row
+        at = self.place
+        for f, copy in enumerate(self.row_copies()):
+            copy.wait_recv()
+            own = summed[aligned(f * 2 + at.row_bit, self.shard), :]
+            other = landed[f * self.shard : (f + 1) * self.shard, :]
+            result[f * self.shard : (f + 1) * self.shard, :] = (
+                own.astype(jnp.float32) + other.astype(jnp.float32)
+            ).astype(result.dtype)
+
+    def line_finish(self):
+        summed, landed, result = self.line
+        at = self.place
+        total = summed[aligned(at.f, self.shard), :].astype(jnp.float32)
+        for step, copy in enumerate(self.line_copies()):
+            copy.wait_recv()
+            total = total + landed[step * self.shard : (step + 1) * self.shard, :].astype(jnp.float32)
+        result[...] = total
+
+    def drain(self, *stages):
+        for stage in stages:
+            for copy in getattr(self, stage + "_copies")():
+                copy.wait_send()
+
+
+def gather_kernel(
+    line,
+    x_ref,
+    pv_own,
+    wo_own,
+    we_own,
+    ws_own,
+    bias_ref,
+    q_ref,
+    kv_ref,
+    pv_ref,
+    wo_ref,
+    we_ref,
+    ws_ref,
+    vec_ref,
+    unit,
+    normed,
+    line_send,
+    line_recv,
+    row_send,
+    row_recv,
+    core_send,
+    core_recv,
+    kv_send,
+    kv_recv,
+):
+    at = Place(line)
+    shard = pv_own.shape[0]
+    rows, width = q_ref.shape
+    half = rows // 2
+    groups = (
+        (pv_own, pv_ref, True),
+        (wo_own, wo_ref, True),
+        (we_own, we_ref, False),
+        (ws_own, ws_ref, False),
+    )
+
+    def block(group, f, ctx):
+        return aligned(f * 4 + ctx if groups[group][2] else f, shard)
+
+    def line_copy(group, f, way, own=False):
+        mine, full, _ = groups[group]
+        part = full.at[block(group, f, at.c), :]
+        return remote(
+            mine if own else part,
+            part,
+            line_send.at[group, (way + 1) // 2, f],
+            line_recv.at[group, f],
+            at.line_device(at.f + way),
+        )
+
+    def row_copy(group, f, own=False):
+        mine, full, _ = groups[group]
+        part = full.at[block(group, f, at.c), :]
+        return remote(
+            mine if own else part, part, row_send.at[group, f], row_recv.at[group, f], at.row_device
+        )
+
+    def core_copy(group, f, other, own=False):
+        mine, full, _ = groups[group]
+        part = full.at[block(group, f, at.row if other else at.c), :]
+        return remote(
+            mine if own else part,
+            part,
+            core_send.at[group, f, other],
+            core_recv.at[group, f, other],
+            at.core_device,
+        )
+
+    def each(step, action):
+        if step == 0:
+            action(at.f, 0)
+            return
+
+        @pl.when(at.f - step >= 0)
+        def _():
+            action(at.f - step, 1)
+
+        @pl.when(at.f + step < line)
+        def _():
+            action(at.f + step, -1)
+
+    def can_pass(way):
+        return at.f < line - 1 if way > 0 else at.f > 0
+
+    def start(group):
+        mine, full, spread = groups[group]
+        for way in (1, -1):
+
+            @pl.when(can_pass(way))
+            def _(way=way):
+                line_copy(group, at.f, way, own=True).start()
+
+        if spread:
+            row_copy(group, at.f, own=True).start()
+            core_copy(group, at.f, 0, own=True).start()
+        full[block(group, at.f, at.c), :] = mine[...]
+
+    def arrive_line(group, f, way):
+        line_copy(group, f, 1).wait_recv()
+
+        @pl.when(can_pass(way))
+        def _():
+            line_copy(group, f, way).start()
+
+        if groups[group][2]:
+            row_copy(group, f).start()
+            core_copy(group, f, 0).start()
+
+    def arrive_row(group, f):
+        row_copy(group, f).wait_recv()
+        core_copy(group, f, 1).start()
+
+    def advance(group):
+        spread = groups[group][2]
+        for step in range(1, line):
+            each(step, lambda f, way: arrive_line(group, f, way))
+            if spread:
+                each(step - 1, lambda f, way: arrive_row(group, f))
+        if spread:
+            each(line - 1, lambda f, way: arrive_row(group, f))
+
+    def finish(group):
+        if groups[group][2]:
+            for f in range(line):
+                for other in (0, 1):
+                    core_copy(group, f, other).wait_recv()
+
+    def drain(group):
+        for step in range(line):
+            for way in (1, -1):
+                source = at.f - step * way
+
+                @pl.when((source >= 0) & (source < line) & can_pass(way))
+                def _(source=source, way=way):
+                    line_copy(group, source, way).wait_send()
+
+        if groups[group][2]:
+            for f in range(line):
+                row_copy(group, f).wait_send()
+                for other in (0, 1):
+                    core_copy(group, f, other).wait_send()
+
+    def kv_row(part):
+        here = kv_ref.at[aligned(at.c * 2 + part, half), :]
+        return remote(here, here, kv_send.at[0, part], kv_recv.at[0, part], at.row_device)
+
+    def kv_core(part, other):
+        here = kv_ref.at[aligned((at.row if other else at.c) * 2 + part, half), :]
+        return remote(
+            here, here, kv_send.at[1 + other, part], kv_recv.at[1 + other, part], at.core_device
+        )
+
+    at.greet(tp=False, line=True)
+    start(0)
+
+    @pl.loop(0, 4)
+    def _(part):
+        these = aligned(part, rows // 4)
+        unit[these, :] = normalize_parts(x_ref[these, :].astype(jnp.float32))[0]
+
+    advance(0)
+    for group in (1, 2, 3):
+        start(group)
+    finish(0)
+    tile = pv_ref.shape[1] - 3 * width
+    vec_ref[...] = pv_ref[:, 3 * width :].astype(jnp.float32).T[0:8, :]
+    gain, shift = vec_ref[0:1, :], vec_ref[1:2, :]
+
+    @pl.loop(0, 4)
+    def _(part):
+        these = aligned(part, rows // 4)
+        normed[these, :] = (unit[these, :] * gain + shift).astype(jnp.bfloat16)
+
+    for part in range(2):
+        left = normed[part * half : (part + 1) * half, :]
+        here = aligned(at.c * 2 + part, half)
+        for piece in range(2):
+            columns = slice((1 + piece) * width, (2 + piece) * width)
+            kv_ref[here, piece * width : (piece + 1) * width] = (
+                dot_nn(left, pv_ref[:, columns]) + bias_ref[:, columns]
+            ).astype(jnp.bfloat16)
+        kv_row(part).start()
+        kv_core(part, 0).start()
+    for part in range(2):
+        these = slice(part * half, (part + 1) * half)
+        q_ref[these, :] = (
+            dot_nn(normed[these, :], pv_ref[:, 0:width]) + bias_ref[:, 0:width]
+        ).astype(jnp.bfloat16)
+    advance(1)
+    advance(2)
+    kv_row(0).wait_recv()
+    kv_core(0, 1).start()
+    advance(3)
+    kv_row(1).wait_recv()
+    kv_core(1, 1).start()
+    for group in (1, 2, 3):
+        finish(group)
+    for part in range(2):
+        for other in range(2):
+            kv_core(part, other).wait_recv()
+    for group in range(4):
+        drain(group)
+    for part in range(2):
+        kv_row(part).wait_send()
+        for other in range(2):
+            kv_core(part, other).wait_send()
+
+
+def lanes_of(pair_head, shape):
+    lane = lax.broadcasted_iota(jnp.int32, shape, 1)
+    return (lane // HEAD_DIM) == pair_head
+
+
+def split_heads(source, store, scale):
+    rows, width = source.shape
+    for pair in range(width // 128):
+        both = source[:, pair * 128 : (pair + 1) * 128].astype(jnp.float32) * scale
+        for side in range(2):
+            store[2 * pair + side, :, :] = jnp.where(
+                lanes_of(side, both.shape), both, 0.0
+            ).astype(jnp.bfloat16)
+
+
+def slot_mask(bias, seg_ref, order_ref, query_slot, key_slot, half):
+    query_seg = seg_ref[:, aligned(query_slot, half, 128)].astype(jnp.float32)
+    key_seg = seg_ref[:, aligned(key_slot, half, 128)].astype(jnp.float32)
+    key_part = jnp.broadcast_to(key_seg, (128, half)).T
+    key_full = jnp.concatenate([key_part] * (half // 128), axis=1)
+    shape = (half, half)
+    key_place = order_ref[0, key_slot] * half + lax.broadcasted_iota(jnp.int32, shape, 0)
+    query_place = order_ref[0, query_slot] * half + lax.broadcasted_iota(jnp.int32, shape, 1)
+    allowed = (key_full == query_seg) & (key_place <= query_place)
+    bias[...] = jnp.where(allowed, 0.0, NEGATIVE)
+
+
+def slot_needed(last_ref, order_ref, query_slot, key_slot, half):
+    query_block, key_block = order_ref[0, query_slot], order_ref[0, key_slot]
+    reaches = last_ref[0, key_slot * half + half - 1] >= query_block * half
+    return (key_block == query_block) | ((key_block < query_block) & reaches)
+
+
+def attend_kernel(
+    q_ref, kv_ref, seg_ref, last_ref, order_ref, out_ref, mixed_ref, lse_ref, heads, bias, top, total
+):
+    rows, width = q_ref.shape
+    half = rows // 2
+    slots = kv_ref.shape[0] // half
+    first = lax.axis_index("ctx") * 2
+    split_heads(q_ref, heads, SCALE)
+    top[...] = jnp.full_like(top, NEGATIVE)
+    total[...] = jnp.zeros_like(total)
+    mixed_ref[...] = jnp.zeros_like(mixed_ref)
+    for part in range(2):
+        these = slice(part * half, (part + 1) * half)
+
+        @pl.loop(0, slots)
+        def _(slot, part=part, these=these):
+            @pl.when(slot_needed(last_ref, order_ref, first + part, slot, half))
+            def _():
+                slot_mask(bias, seg_ref, order_ref, first + part, slot, half)
+                keys = aligned(slot, half)
+                for head in range(width // HEAD_DIM):
+                    pair, side = head // 2, head % 2
+                    scores = (
+                        dot_nt(kv_ref[keys, pair * 128 : (pair + 1) * 128], heads[head, these, :])
+                        + bias[...]
+                    )
+                    before = top[head : head + 1, these]
+                    after = jnp.maximum(before, jnp.max(scores, axis=0, keepdims=True))
+                    raised = jnp.exp(scores - after)
+                    fade = jnp.exp(before - after)
+                    top[head : head + 1, these] = after
+                    total[head : head + 1, these] = total[head : head + 1, these] * fade + jnp.sum(
+                        raised, axis=0, keepdims=True
+                    )
+                    value = kv_ref[keys, width + pair * 128 : width + (pair + 1) * 128].T
+                    spot = slice(head * HEAD_DIM, (head + 1) * HEAD_DIM)
+                    mixed_ref[spot, these] = mixed_ref[spot, these] * fade + dot_nn(
+                        value[side * HEAD_DIM : (side + 1) * HEAD_DIM, :],
+                        raised.astype(jnp.bfloat16),
+                    )
+
+    for head in range(width // HEAD_DIM):
+        spot = slice(head * HEAD_DIM, (head + 1) * HEAD_DIM)
+        mixed_ref[spot, :] = mixed_ref[spot, :] / total[head : head + 1, :]
+    for pair in range(width // 128):
+        span = slice(pair * 128, (pair + 1) * 128)
+        out_ref[:, span] = mixed_ref[span, :].T.astype(jnp.bfloat16)
+    lse_ref[...] = top[...] + jnp.log(total[...])
+
+
+def attend_back_kernel(
+    q_ref,
+    kv_ref,
+    slope_ref,
+    mixed_ref,
+    lse_ref,
+    seg_ref,
+    last_ref,
+    order_ref,
+    dq_ref,
+    dkv_ref,
+    heads,
+    slopes,
+    bias,
+    delta,
+    dq_sum,
+    dkv_sum,
+):
+    rows, width = q_ref.shape
+    half = rows // 2
+    slots = kv_ref.shape[0] // half
+    first = lax.axis_index("ctx") * 2
+    split_heads(q_ref, heads, SCALE)
+    split_heads(slope_ref, slopes, 1.0)
+    dq_sum[...] = jnp.zeros_like(dq_sum)
+    for pair in range(width // 128):
+        span = slice(pair * 128, (pair + 1) * 128)
+        product = slope_ref[:, span].astype(jnp.float32).T * mixed_ref[span, :]
+        for side in range(2):
+            head = 2 * pair + side
+            delta[head : head + 1, :] = jnp.sum(
+                product[side * HEAD_DIM : (side + 1) * HEAD_DIM, :], axis=0, keepdims=True
+            )
+
+    @pl.loop(0, slots)
+    def _(slot):
+        keys = aligned(slot, half)
+        dkv_sum[...] = jnp.zeros_like(dkv_sum)
+        for part in range(2):
+            these = slice(part * half, (part + 1) * half)
+
+            @pl.when(slot_needed(last_ref, order_ref, first + part, slot, half))
+            def _(part=part, these=these):
+                slot_mask(bias, seg_ref, order_ref, first + part, slot, half)
+                for pair in range(width // 128):
+                    span = slice(pair * 128, (pair + 1) * 128)
+                    value_span = slice(width + pair * 128, width + (pair + 1) * 128)
+                    key = kv_ref[keys, span]
+                    value = kv_ref[keys, value_span]
+                    key_turned = key.T
+                    for side in range(2):
+                        head = 2 * pair + side
+                        scores = dot_nt(key, heads[head, these, :]) + bias[...]
+                        chance = jnp.exp(scores - lse_ref[head : head + 1, these])
+                        pulled = dot_nt(value, slopes[head, these, :])
+                        slope = (chance * (pulled - delta[head : head + 1, these])).astype(
+                            jnp.bfloat16
+                        )
+                        dkv_sum[:, value_span] += dot_nn(
+                            chance.astype(jnp.bfloat16), slopes[head, these, :]
+                        )
+                        dkv_sum[:, span] += dot_nn(slope, heads[head, these, :])
+                        spot = slice(head * HEAD_DIM, (head + 1) * HEAD_DIM)
+                        dq_sum[spot, these] += dot_nn(
+                            key_turned[side * HEAD_DIM : (side + 1) * HEAD_DIM, :], slope
+                        )
+
+        dkv_ref[keys, :] = dkv_sum[...].astype(jnp.bfloat16)
+
+    for pair in range(width // 128):
+        span = slice(pair * 128, (pair + 1) * 128)
+        dq_ref[:, span] = (dq_sum[span, :] * SCALE).T.astype(jnp.bfloat16)
+
+
+def gelu_both(v):
+    square = v * v
+    inner = GELU_A * v * (1.0 + GELU_B * square)
+    bent = jnp.tanh(inner)
+    lifted = 0.5 * (1.0 + bent)
+    slope = lifted + 0.5 * v * (1.0 - bent * bent) * (GELU_A * (1.0 + 3.0 * GELU_B * square))
+    return (v * lifted, slope)
+
+
+def middle_kernel(
+    line,
+    att_ref,
+    x_ref,
+    ct_ref,
+    wo_ref,
+    we_part,
+    ws_part,
+    vec_ref,
+    bias_ref,
+    mid_ref,
+    mids_ref,
+    att_slope_ref,
+    feed_ref,
+    shrink_ref,
+    expand_ref,
+    go_ref,
+    vsum_ref,
+    bsum_ref,
+    we,
+    ws,
+    out_send,
+    out_land,
+    up_send,
+    up_land,
+    normed,
+    active,
+    before_slope,
+    turned,
+    gs,
+    ge,
+    gs_land,
+    ge_land,
+    gs_sum,
+    gs_land2,
+    row_send,
+    row_recv,
+    core_send,
+    core_recv,
+    tp_send,
+    tp_recv,
+    *sems,
+):
+    at = Place(line)
+    shard = we_part.shape[0] // line
+    rows, model = x_ref.shape
+    hidden = we.shape[1]
+    pieces = 4
+    some = rows // pieces
+    groups = ((we_part, we), (ws_part, ws))
+
+    def row_copy(group, f):
+        part, full = groups[group]
+        return remote(
+            part.at[pl.ds(f * shard, shard), :],
+            full.at[aligned(f * 4 + at.c, shard), :],
+            row_send.at[group, f],
+            row_recv.at[group, f],
+            at.row_device,
+        )
+
+    def core_copy(group, f, other):
+        part, full = groups[group]
+        there = full.at[aligned(f * 4 + (at.row if other else at.c), shard), :]
+        return remote(
+            there if other else part.at[pl.ds(f * shard, shard), :],
+            there,
+            core_send.at[group, f, other],
+            core_recv.at[group, f, other],
+            at.core_device,
+        )
+
+    def tp_copy(kind, piece):
+        source, target = ((out_send, out_land), (up_send, up_land))[kind]
+        these = aligned(piece, some)
+        return remote(
+            source.at[these, :],
+            target.at[these, :],
+            tp_send.at[kind, piece],
+            tp_recv.at[kind, piece],
+            at.tp_device,
+        )
+
+    shrink = Scatter(
+        at, 0, shard, sems, core=(gs, gs_land, gs_sum), row=(gs_sum, gs_land2, shrink_ref)
+    )
+    expand = Scatter(at, 1, shard, sems, core=(ge, ge_land, expand_ref))
+
+    at.greet(tp=True, line=False)
+    for group in range(2):
+        for f in range(line):
+            row_copy(group, f).start()
+    for group in range(2):
+        part, full = groups[group]
+        for f in range(line):
+            core_copy(group, f, 0).start()
+            full[aligned(f * 4 + at.c, shard), :] = part[f * shard : (f + 1) * shard, :]
+
+    @pl.loop(0, pieces)
+    def _(piece):
+        these = aligned(piece, some)
+        out_send[these, :] = dot_nt(att_ref[these, :], wo_ref[...]).astype(jnp.bfloat16)
+        tp_copy(0, piece).start()
+
+    for group in range(2):
+        for f in range(line):
+            row_copy(group, f).wait_recv()
+            core_copy(group, f, 1).start()
+    for group in range(2):
+        for f in range(line):
+            for other in range(2):
+                core_copy(group, f, other).wait_recv()
+    out_bias, gain, shift = vec_ref[2:3, :], vec_ref[3:4, :], vec_ref[4:5, :]
+
+    @pl.loop(0, pieces)
+    def _(piece):
+        these = aligned(piece, some)
+        tp_copy(0, piece).wait_recv()
+        branch = out_send[these, :].astype(jnp.float32) + out_land[these, :].astype(jnp.float32)
+        middle = x_ref[these, :].astype(jnp.float32) + branch + out_bias
+        mid_ref[these, :] = middle
+        unit, _ = normalize_parts(middle)
+        low = (unit * gain + shift).astype(jnp.bfloat16)
+        normed[these, :] = low
+        for column in range(0, hidden, 512):
+            span = slice(column, column + 512)
+            value, slope = gelu_both(dot_nn(low, we[:, span]) + bias_ref[:, span])
+            active[these, span] = value.astype(jnp.bfloat16)
+            before_slope[these, span] = (dot_nn(ct_ref[these, :], ws[:, span]) * slope).astype(
+                jnp.bfloat16
+            )
+        up_send[these, :] = dot_nt(before_slope[these, :], we[...]).astype(jnp.bfloat16)
+        tp_copy(1, piece).start()
+
+    turned[...] = ct_ref[...].T
+    for column in range(0, hidden, 512):
+        span = slice(column, column + 512)
+        gs[:, span] = dot_nn(turned[...], active[:, span]).astype(jnp.bfloat16)
+    shrink.start("core")
+    turned[...] = normed[...].T
+    for column in range(0, hidden, 512):
+        span = slice(column, column + 512)
+        ge[:, span] = dot_nn(turned[...], before_slope[:, span]).astype(jnp.bfloat16)
+    expand.start("core")
+    shrink.core_finish()
+    shrink.start("row")
+
+    @pl.loop(0, pieces)
+    def _(piece):
+        these = aligned(piece, some)
+        feed_ref[these, :] = dot_nt(active[these, :], ws[...]).astype(jnp.bfloat16)
+
+    bsum_ref[...] = jnp.sum(before_slope[...].astype(jnp.float32), axis=0, keepdims=True)
+    expand.core_finish()
+    vsum_ref[...] = jnp.zeros_like(vsum_ref)
+
+    @pl.loop(0, pieces)
+    def _(piece):
+        these = aligned(piece, some)
+        tp_copy(1, piece).wait_recv()
+        upstream = up_send[these, :].astype(jnp.float32) + up_land[these, :].astype(jnp.float32)
+        unit, inverse = normalize_parts(mid_ref[these, :])
+        back, gain_delta, shift_delta = norm_backward(upstream, unit, inverse, gain)
+        slope = ct_ref[these, :].astype(jnp.float32)
+        middle_slope = slope + back
+        mids_ref[these, :] = middle_slope
+        vsum_ref[2:3, :] += jnp.sum(middle_slope, axis=0, keepdims=True)
+        vsum_ref[3:4, :] += gain_delta[None]
+        vsum_ref[4:5, :] += shift_delta[None]
+        vsum_ref[5:6, :] += jnp.sum(slope, axis=0, keepdims=True)
+        low = middle_slope.astype(jnp.bfloat16)
+        normed[these, :] = low
+        att_slope_ref[these, :] = dot_nn(low, wo_ref[...]).astype(jnp.bfloat16)
+
+    turned[...] = normed[...].T
+    go_ref[...] = dot_nn(turned[...], att_ref[...]).astype(jnp.bfloat16)
+    shrink.row_finish()
+    for group in range(2):
+        for f in range(line):
+            row_copy(group, f).wait_send()
+            for other in range(2):
+                core_copy(group, f, other).wait_send()
+    for kind in range(2):
+        for piece in range(pieces):
+            tp_copy(kind, piece).wait_send()
+    shrink.drain("core", "row")
+    expand.drain("core")
+
+
+def last_kernel(
+    line,
+    dq_ref,
+    dkv_ref,
+    x_ref,
+    pv_ref,
+    mids_ref,
+    mid_ref,
+    feed_ref,
+    ts_ref,
+    se_ref,
+    go_ref,
+    vec_ref,
+    vsum_ref,
+    bsum_ref,
+    out_ref,
+    delta_ref,
+    gs_out,
+    ge_out,
+    go_out,
+    gp_out,
+    gv_out,
+    bias_out,
+    kv_land,
+    kv_pass,
+    kv_land2,
+    kv_low,
+    back,
+    down_send,
+    down_land,
+    feed_land,
+    normed,
+    turned,
+    vec_sum,
+    te,
+    te_land,
+    go_land,
+    go_sum,
+    go_land2,
+    to,
+    gp,
+    gp_land,
+    gp_sum,
+    gp_land2,
+    tp_part,
+    gv,
+    gv_land,
+    gv_sum,
+    gv_land2,
+    tv,
+    zs,
+    ze,
+    zo,
+    zp,
+    zv,
+    bias_pack,
+    bias_land,
+    bias_line,
+    kv_send,
+    kv_recv,
+    tp_send,
+    tp_recv,
+    bias_send,
+    bias_recv,
+    *sems,
+):
+    at = Place(line)
+    rows, width = dq_ref.shape
+    half = rows // 2
+    shard = ts_ref.shape[0] // line
+    pieces = 4
+    some = rows // pieces
+    hidden = ts_ref.shape[1]
+
+    shrink = Scatter(at, 0, shard, sems, line=(ts_ref, zs, gs_out))
+    expand = Scatter(at, 1, shard, sems, row=(se_ref, te_land, te), line=(te, ze, ge_out))
+    output = Scatter(
+        at,
+        2,
+        shard,
+        sems,
+        core=(go_ref, go_land, go_sum),
+        row=(go_sum, go_land2, to),
+        line=(to, zo, go_out),
+    )
+    project = Scatter(
+        at,
+        3,
+        shard,
+        sems,
+        core=(gp, gp_land, gp_sum),
+        row=(gp_sum, gp_land2, tp_part),
+        line=(tp_part, zp, gp_out),
+    )
+    vector = Scatter(
+        at,
+        4,
+        shard,
+        sems,
+        core=(gv, gv_land, gv_sum),
+        row=(gv_sum, gv_land2, tv),
+        line=(tv, zv, gv_out),
+    )
+
+    def kv_core(y, part):
+        return remote(
+            dkv_ref.at[aligned((2 * y + 1 - at.core_bit) * 2 + part, half), :],
+            kv_land.at[aligned(y * 2 + part, half), :],
+            kv_send.at[0, y, part],
+            kv_recv.at[0, y, part],
+            at.core_device,
+        )
+
+    def kv_row(part):
+        return remote(
+            kv_pass.at[pl.ds(part * half, half), :],
+            kv_land2.at[pl.ds(part * half, half), :],
+            kv_send.at[1, 0, part],
+            kv_recv.at[1, 0, part],
+            at.row_device,
+        )
+
+    def tp_copy(kind, piece):
+        source, target = ((feed_ref, feed_land), (down_send, down_land))[kind]
+        these = aligned(piece, some)
+        return remote(
+            source.at[these, :],
+            target.at[these, :],
+            tp_send.at[kind, piece],
+            tp_recv.at[kind, piece],
+            at.tp_device,
+        )
+
+    at.greet(tp=True, line=True)
+    far, near = 1 - at.row_bit, at.row_bit
+    for y in (far, near):
+        for part in range(2):
+            kv_core(y, part).start()
+    for piece in range(pieces):
+        tp_copy(0, piece).start()
+    shrink.start("line")
+    output.start("core")
+    for part in range(2):
+        kv_core(far, part).wait_recv()
+        mine = dkv_ref[aligned((2 * far + at.core_bit) * 2 + part, half), :].astype(jnp.float32)
+        landed = kv_land[aligned(far * 2 + part, half), :].astype(jnp.float32)
+        kv_pass[part * half : (part + 1) * half, :] = (mine + landed).astype(jnp.bfloat16)
+        kv_row(part).start()
+    expand.start("row")
+    output.core_finish()
+    output.start("row")
+    gain, shift = vec_ref[0:1, :], vec_ref[1:2, :]
+
+    @pl.loop(0, pieces)
+    def _(piece):
+        these = aligned(piece, some)
+        unit, _ = normalize_parts(x_ref[these, :].astype(jnp.float32))
+        normed[these, :] = (unit * gain + shift).astype(jnp.bfloat16)
+        back[these, :] = dot_nt(dq_ref[these, :], pv_ref[:, 0:width])
+
+    turned[...] = normed[...].T
+    gp[:, 0:width] = dot_nn(turned[...], dq_ref[...]).astype(jnp.bfloat16)
+    shrink_bias = vec_ref[5:6, :]
+
+    @pl.loop(0, pieces)
+    def _(piece):
+        these = aligned(piece, some)
+        tp_copy(0, piece).wait_recv()
+        feed = (
+            feed_ref[these, :].astype(jnp.float32) + feed_land[these, :].astype(jnp.float32)
+        ).astype(jnp.bfloat16)
+        out_ref[these, :] = (mid_ref[these, :] + feed.astype(jnp.float32) + shrink_bias).astype(
+            jnp.bfloat16
+        )
+
+    for part in range(2):
+        kv_core(near, part).wait_recv()
+        kv_row(part).wait_recv()
+        these = slice(part * half, (part + 1) * half)
+        total = dkv_ref[aligned(at.c * 2 + part, half), :].astype(jnp.float32)
+        total = total + kv_land[aligned(near * 2 + part, half), :].astype(jnp.float32)
+        total = total + kv_land2[these, :].astype(jnp.float32)
+        kv_low[these, :] = total.astype(jnp.bfloat16)
+        for step in range(pieces // 2):
+            piece = part * (pieces // 2) + step
+            these = slice(piece * some, (piece + 1) * some)
+            down_send[these, :] = (
+                back[these, :] + dot_nt(kv_low[these, :], pv_ref[:, width : 3 * width])
+            ).astype(jnp.bfloat16)
+            tp_copy(1, piece).start()
+    for piece in range(2):
+        span = slice((1 + piece) * width, (2 + piece) * width)
+        gp[:, span] = dot_nn(
+            turned[...], kv_low[:, piece * width : (piece + 1) * width]
+        ).astype(jnp.bfloat16)
+    project.start("core")
+    bias_row = jnp.concatenate(
+        [
+            bsum_ref[...],
+            jnp.sum(dq_ref[...].astype(jnp.float32), axis=0, keepdims=True),
+            jnp.sum(kv_low[:, width:].astype(jnp.float32), axis=0, keepdims=True),
+        ],
+        axis=1,
+    )
+    bias_pack[...] = jnp.zeros_like(bias_pack)
+    for index in range(bias_row.shape[1] // 128):
+        bias_pack[0, index : index + 1, :] = bias_row[:, index * 128 : (index + 1) * 128]
+
+    def bias_copy(stage):
+        device = (at.core_device, at.row_device)[stage]
+        return remote(
+            bias_pack.at[stage],
+            bias_land.at[stage],
+            bias_send.at[0, stage],
+            bias_recv.at[0, stage],
+            device,
+        )
+
+    def bias_line_copy(step):
+        target = lax.rem(at.f + step, line)
+        return remote(
+            bias_pack.at[2],
+            bias_line.at[at.f],
+            bias_send.at[1, step],
+            bias_recv.at[1, step],
+            at.line_device(target),
+        )
+
+    bias_copy(0).start()
+    expand.row_finish()
+    expand.start("line")
+    output.row_finish()
+    output.start("line")
+    project.core_finish()
+    project.start("row")
+    bias_copy(0).wait_recv()
+    bias_pack[1, :, :] = bias_pack[0, :, :] + bias_land[0, :, :]
+    bias_copy(1).start()
+    shrink.line_finish()
+    bias_copy(1).wait_recv()
+    bias_pack[2, :, :] = bias_pack[1, :, :] + bias_land[1, :, :]
+    for step in range(1, line):
+        bias_line_copy(step).start()
+    vec_sum[...] = jnp.zeros_like(vec_sum)
+    vec_sum[0:8, :] = vsum_ref[...]
+
+    @pl.loop(0, pieces)
+    def _(piece):
+        these = aligned(piece, some)
+        tp_copy(1, piece).wait_recv()
+        upstream = down_send[these, :].astype(jnp.float32) + down_land[these, :].astype(jnp.float32)
+        unit, inverse = normalize_parts(x_ref[these, :].astype(jnp.float32))
+        slope, gain_delta, shift_delta = norm_backward(upstream, unit, inverse, gain)
+        delta_ref[these, :] = mids_ref[these, :] + slope
+        vec_sum[0:1, :] += gain_delta[None]
+        vec_sum[1:2, :] += shift_delta[None]
+
+    gv[...] = vec_sum[...].T.astype(jnp.bfloat16)
+    vector.start("core")
+    project.row_finish()
+    project.start("line")
+    vector.core_finish()
+    vector.start("row")
+    expand.line_finish()
+    output.line_finish()
+    vector.row_finish()
+    vector.start("line")
+    for step in range(1, line):
+        source = lax.rem(at.f + line - step, line)
+        remote(
+            bias_pack.at[2],
+            bias_line.at[source],
+            bias_send.at[1, step],
+            bias_recv.at[1, step],
+            at.row_device,
+        ).wait_recv()
+    bias_line[at.f, :, :] = bias_pack[2, :, :]
+    total = bias_line[0, :, :]
+    for f in range(1, line):
+        total = total + bias_line[f, :, :]
+    bias_out[...] = total
+    project.line_finish()
+    vector.line_finish()
+    for y in range(2):
+        for part in range(2):
+            kv_core(y, part).wait_send()
+    for part in range(2):
+        kv_row(part).wait_send()
+    for kind in range(2):
+        for piece in range(pieces):
+            tp_copy(kind, piece).wait_send()
+    for stage in range(2):
+        bias_copy(stage).wait_send()
+    for step in range(1, line):
+        bias_line_copy(step).wait_send()
+    shrink.drain("line")
+    expand.drain("row", "line")
+    output.drain("core", "row", "line")
+    project.drain("core", "row", "line")
+    vector.drain("core", "row", "line")
+
+
+def whole(count, space=None):
+    return [pl.BlockSpec(memory_space=space or pltpu.VMEM)] * count
+
+
+def call(kernel, outs, scratch, args, spaces=None, identity=None):
+    params = dict(vmem_limit_bytes=VMEM_BYTES)
+    if identity is not None:
+        params.update(collective_id=identity, has_side_effects=True)
+    return pl.pallas_call(
+        kernel,
+        out_shape=[jax.ShapeDtypeStruct(shape, dtype) for shape, dtype in outs],
+        in_specs=spaces or whole(len(args)),
+        out_specs=whole(len(outs)),
+        scratch_shapes=scratch,
+        compiler_params=pltpu.CompilerParams(**params),
+    )(*args)
+
+
+def buffers(*shapes):
+    return [pltpu.VMEM(shape, dtype) for shape, dtype in shapes]
+
+
+def dma(*shape):
+    return pltpu.SemaphoreType.DMA(shape)
+
+
+def scatter_sems(count, line):
+    return [dma(count, n) for n in (2 * line, 2 * line, line, line, line, line)]
+
+
+def by_kernels(
+    layer_input,
+    cotangent,
+    segments,
+    slot_order,
+    first_gain,
+    first_shift,
+    project_weight,
+    project_bias,
+    output_weight,
+    output_bias,
+    second_gain,
+    second_shift,
+    expand_weight,
+    expand_bias,
+    shrink_weight,
+    shrink_bias,
+):
+    low, full = jnp.bfloat16, jnp.float32
+    line = lax.axis_size("fsdp")
+    _, rows, model = layer_input.shape
+    length = segments.shape[1]
+    slots = slot_order.shape[1]
+    shard, _, width = project_weight.shape
+    hidden = expand_weight.shape[1]
+    count = width // HEAD_DIM
+    half = rows // 2
+    x = layer_input.reshape(rows, model)
+    ct = cotangent.reshape(rows, model)
+    vectors = jnp.stack(
+        [first_gain, first_shift, output_bias, second_gain, second_shift, shrink_bias], axis=1
+    )
+    pv_own = jnp.concatenate(
+        [project_weight.reshape(shard, 3 * width), jnp.pad(vectors, ((0, 0), (0, 122)))], axis=1
+    )
+    zero = jnp.zeros((width,), full)
+    qkv_bias = jnp.concatenate(
+        [project_bias[0].astype(full), zero, project_bias[1].astype(full)]
+    ).reshape(1, 3 * width)
+    packed = pv_own.shape[1]
+    q, kv, pv, wo, we_part, ws_part, vec = call(
+        partial(gather_kernel, line),
+        [
+            ((rows, width), low),
+            ((length, 2 * width), low),
+            ((model, packed), low),
+            ((model, width), low),
+            ((line * shard, hidden), low),
+            ((line * shard, hidden), low),
+            ((8, model), full),
+        ],
+        buffers(((rows, model), full), ((rows, model), low))
+        + [
+            dma(4, 2, line),
+            dma(4, line),
+            dma(2, line),
+            dma(2, line),
+            dma(2, line, 2),
+            dma(2, line, 2),
+            dma(3, 2),
+            dma(3, 2),
+        ],
+        (x, pv_own, output_weight.T, expand_weight, shrink_weight.T, qkv_bias),
+        identity=0,
+    )
+    tables = (segments, segments, slot_order)
+    table_spaces = whole(1) + whole(2, pltpu.SMEM)
+    att, mixed, lse = call(
+        attend_kernel,
+        [((rows, width), low), ((width, rows), full), ((8, rows), full)],
+        buffers(
+            ((count, rows, 128), low), ((half, half), full), ((8, rows), full), ((8, rows), full)
+        ),
+        (q, kv, *tables),
+        spaces=whole(2) + table_spaces,
+    )
+    mid, mids, att_slope, feed, ts, se, go, vsum, bsum = call(
+        partial(middle_kernel, line),
+        [
+            ((rows, model), full),
+            ((rows, model), full),
+            ((rows, width), low),
+            ((rows, model), low),
+            ((line * shard, hidden), low),
+            ((2 * line * shard, hidden), low),
+            ((model, width), low),
+            ((8, model), full),
+            ((1, hidden), full),
+        ],
+        buffers(
+            ((model, hidden), low),
+            ((model, hidden), low),
+            ((rows, model), low),
+            ((rows, model), low),
+            ((rows, model), low),
+            ((rows, model), low),
+            ((rows, model), low),
+            ((rows, hidden), low),
+            ((rows, hidden), low),
+            ((model, rows), low),
+            ((model, hidden), low),
+            ((model, hidden), low),
+            ((2 * line * shard, hidden), low),
+            ((2 * line * shard, hidden), low),
+            ((2 * line * shard, hidden), low),
+            ((line * shard, hidden), low),
+        )
+        + [
+            dma(2, line),
+            dma(2, line),
+            dma(2, line, 2),
+            dma(2, line, 2),
+            dma(2, 4),
+            dma(2, 4),
+        ]
+        + scatter_sems(2, line),
+        (att, x, ct, wo, we_part, ws_part, vec, expand_bias.astype(full).reshape(1, hidden)),
+        identity=1,
+    )
+    dq, dkv = call(
+        attend_back_kernel,
+        [((rows, width), low), ((length, 2 * width), low)],
+        buffers(
+            ((count, rows, 128), low),
+            ((count, rows, 128), low),
+            ((half, half), full),
+            ((8, rows), full),
+            ((width, rows), full),
+            ((half, 2 * width), full),
+        ),
+        (q, kv, att_slope, mixed, lse, *tables),
+        spaces=whole(5) + table_spaces,
+    )
+    two, one = 2 * line * shard, line * shard
+    less = one - shard
+    bias_rows = -(-(hidden + 2 * width) // 1024) * 8
+
+    def stages(columns, *kinds):
+        size = {"full": model, "two": two, "one": one, "less": less}
+        return [((size[kind], columns), low) for kind in kinds]
+
+    out, delta, gs, ge, go, gp, gv, biases = call(
+        partial(last_kernel, line),
+        [
+            ((rows, model), low),
+            ((rows, model), full),
+            ((shard, hidden), full),
+            ((shard, hidden), full),
+            ((shard, width), full),
+            ((shard, 3 * width), full),
+            ((shard, 128), full),
+            ((bias_rows, 128), full),
+        ],
+        buffers(
+            ((2 * rows, 2 * width), low),
+            ((rows, 2 * width), low),
+            ((rows, 2 * width), low),
+            ((rows, 2 * width), low),
+            ((rows, model), full),
+            ((rows, model), low),
+            ((rows, model), low),
+            ((rows, model), low),
+            ((rows, model), low),
+            ((model, rows), low),
+            ((128, model), full),
+            *stages(hidden, "one", "one"),
+            *stages(width, "two", "two", "one", "one"),
+            *stages(3 * width, "full", "two", "two", "one", "one"),
+            *stages(128, "full", "two", "two", "one", "one"),
+            *stages(hidden, "less", "less"),
+            *stages(width, "less"),
+            *stages(3 * width, "less"),
+            *stages(128, "less"),
+            ((3, bias_rows, 128), full),
+            ((2, bias_rows, 128), full),
+            ((line, bias_rows, 128), full),
+        )
+        + [dma(2, 2, 2), dma(2, 2, 2), dma(2, 4), dma(2, 4), dma(2, line), dma(2, line)]
+        + scatter_sems(5, line),
+        (dq, dkv, x, pv, mids, mid, feed, ts, se, go, vec, vsum, bsum),
+        identity=2,
+    )
+    biases = biases.reshape(-1)
+    return (
+        out.reshape(layer_input.shape),
+        delta.reshape(layer_input.shape),
+        gv[:, 0],
+        gv[:, 1],
+        gp.reshape(shard, 3, width),
+        biases[hidden : hidden + 2 * width].reshape(2, width),
+        go.T,
+        gv[:, 2],
+        gv[:, 3],
+        gv[:, 4],
+        ge,
+        biases[:hidden],
+        gs.T,
+        gv[:, 5],
+    )
+
+
 def solution(mesh):
+    n_ctx, n_tp = mesh.shape["ctx"], mesh.shape["tp"]
+
+    def choose(layer_input, *others):
+        seqs, rows, model = layer_input.shape
+        whole_tiles = model % (16 * n_ctx * mesh.shape["fsdp"]) == 0 and rows % 256 == 0
+        if seqs == 1 and n_ctx == 4 and n_tp == 2 and whole_tiles:
+            return by_kernels(layer_input, *others)
+        return on_device(layer_input, *others)
+
     return jax.shard_map(
-        on_device,
+        choose,
         mesh=mesh,
         in_specs=(
             P("fsdp", "ctx", None),

time: 801 us -> 242 us (0.30)
  waiting for transfers between devices: 390 us -> 0 us
  Pallas kernels: 0 us -> 224 us
  blocking collectives: 167 us -> 0 us
  matrix products: 94.3 us -> 0 us
  other arithmetic: 72.5 us -> 1.44 us
  local copies, waits for them, and re-layouts: 52.9 us -> 15 us
  between operations: 17.1 us -> 0.71 us
    pallas_call x0 -> x5, Pallas kernels: none -> 224 us  [call(): pl.pallas_call(kernel, out_shape=[jax.ShapeDtypeStruct(shape, dtype) for...]
    reduce_scatter x10 -> x0, waiting for transfers between devices: 215 us -> none  [the longest x1 48.6 us: on_device(): lax.psum_scatter(expand_weight_delta.astype(jnp.bfloat16), 'fsdp', scatte...]
    dot_general x33 -> x0, matrix products: 94.3 us -> none  [the longest x6 23.5 us: masked_scores(): jnp.einsum('qhd,khd->hqk', query_heads, key_heads, preferred_element_type...]
    all_gather x5 -> x0, waiting for transfers between devices: 94.2 us -> none  [the longest x1 41 us: on_device(): lax.all_gather(expand_weight, ('fsdp', 'ctx'), axis=0, tiled=True)]
    unnamed x3 -> x0, blocking collectives: 86.8 us -> none
    psum x3 -> x0, waiting for transfers between devices: 78.4 us -> none  [the longest x1 45.2 us: on_device(): lax.psum(jnp.dot(attended_flat, output_full, preferred_element_type=jnp.f...]
    psum x1 -> x0, blocking collectives: 59.5 us -> none  [on_device(): lax.psum((project_bias_delta, expand_bias_delta), ('fsdp', 'ctx'))]
    convert_element_type x22 -> x1, other arithmetic: 36.9 us -> 0.77 us  [by_kernels(): project_bias[0].astype(full)]
  transfers between devices with their start and end apart: 18 -> 0, of which waited for: 14 -> 0; matrix products, arithmetic and copies ran while one was open for 19% -> 0% of each run, Pallas kernels for 0% -> 0%
where the time goes in v1:
time: 242 us; the launch traced here: 241 us
  Pallas kernels  224 us (93%)
  local copies, waits for them, and re-layouts  15 us (6%)
    pallas_call x5, Pallas kernels, call(): pl.pallas_call(kernel, out_shape=[jax.ShapeDtypeStruct(shape, dtype) for...  224 us
    unnamed x13, local copies, waits for them, and re-layouts  5.28 us

profile of v1, /device:TPU:0, one launch (start us, length us, event | category | flops | bytes accessed | tf_op | source)
XLA Modules:
  0.0 241.2 jit_solution(18252890791073621743)
XLA Ops:
  0.6 0.8 stack.27
  1.4 0.8 convert_reduce_fusion.1
  2.2 0.6 reshape.67.bias_ref
  2.8 1.3 reshape.78.bias_ref
  4.1 0.1 copy.47
  4.2 0.9 copy.50
  5.1 0.7 fusion.1.pv_own
  5.8 62.7 %shard_map.263 = (bf16[512,384]{1,0:T(8,128)(2,1)}, bf16[2048,768]{1,0:T(8,128)(2,1)}, bf16[768,1280]{1,0:T(8,128)(2,1)}, bf16[768,384]{1,0:T(8,128)(2,1)}, bf16...) custom-call(bf16[512,768]{1,0:T(8,128)(2,1)} %bitcast.22, bf16[48,1280]{1,0:T(8,128)(2,1)} %fusion.1.pv_own, ...), custom_call_target="tpu_custom_call" | custom-call | tf_op jit(solution)/shard_map/pallas_call | solution.py:1503
  68.5 14.3 %shard_map.264 = (bf16[512,384]{1,0:T(8,128)(2,1)}, f32[384,512]{1,0:T(8,128)}, f32[8,512]{1,0:T(8,128)}) custom-call(bf16[512,384]{1,0:T(8,128)(2,1)} %get-tuple-element.43.q_ref, bf16[2048,768]{1,0:T(8,128)(2,1)} %get-tuple-element.44.kv_ref, s32[1,2048]{1,0:T(1,128)} %last_ref.3, s32[1,2048]{1,0:T(1,128)} %last_ref.3, s32[1,8]{1,0:T(1,128)} %order_ref.3), custom_call_target="tpu_custom_call" | custom-call | tf_op jit(solution)/shard_map/pallas_call | solution.py:1503
  82.8 59.8 %shard_map.265 = (f32[512,768]{1,0:T(8,128)}, f32[512,768]{1,0:T(8,128)}, bf16[512,384]{1,0:T(8,128)(2,1)}, bf16[512,768]{1,0:T(8,128)(2,1)}, bf16[192,1536]{1,0...) custom-call(bf16[512,384]{1,0:T(8,128)(2,1)} %get-tuple-element.45.a, ...), custom_call_target="tpu_custom_call" | custom-call | tf_op jit(solution)/shard_map/pallas_call | solution.py:1503
  142.7 15.0 %shard_map.266 = (bf16[512,384]{1,0:T(8,128)(2,1)}, bf16[2048,768]{1,0:T(8,128)(2,1)}) custom-call(bf16[512,384]{1,0:T(8,128)(2,1)} %get-tuple-element.43.q_ref, bf16[2048,768]{1,0:T(8,128)(2,1)} %get-tuple-element.44.kv_ref, bf16[512,384]{1,0:T(8,128)(2,1)} %get-tuple-element.50.slope_ref, f32[384,512]{1,0:T(8,128)} %get-tuple-element.51.mixed_ref, ...), custom_call_target="tpu_custom_call" | custom-call | tf_op jit(solution)/shard_map/pallas_call | solution.py:1503
  157.7 72.2 %shard_map.267 = (bf16[512,768]{1,0:T(8,128)(2,1)}, f32[512,768]{1,0:T(8,128)}, f32[48,1536]{1,0:T(8,128)}, f32[48,1536]{1,0:T(8,128)}, f32[48,384]{1,0:T(8,128)...) custom-call(bf16[512,384]{1,0:T(8,128)(2,1)} %get-tuple-element.53.dq_ref, ...), custom_call_target="tpu_custom_call" | custom-call | tf_op jit(solution)/shard_map/pallas_call | solution.py:1503
  229.8 0.0 copy-start
  229.9 1.9 slice_reduce_fusion
  231.7 0.7 slice.38
  232.4 1.3 slice_bitcast_fusion
  233.7 0.6 reshape.74
  234.3 1.6 copy.52
  236.0 2.1 copy.58
  238.0 0.0 copy-done
  238.0 0.0 copy-start.3
  238.0 0.0 copy-start.2
  238.0 0.0 copy-start.1
  238.0 1.1 copy.59
  239.2 0.0 copy-done.3
  239.2 0.6 copy.60
  239.8 0.0 copy-done.2
  239.8 0.7 copy.61
  240.5 0.0 copy-done.1
  240.5 0.7 copy.62
  (2 shorter events, 0.0 us)
Async XLA Ops:
  229.8 8.2 %copy-start = (f32[512,768]{1,0:T(8,128)S(1)}, f32[512,768]{1,0:T(8,128)}, u32[]{:S(2)}) copy-start(f32[512,768]{1,0:T(8,128)} %get-tuple-element.65) | copy-start | bytes 4718596
  238.0 1.2 copy-start.3
  238.0 1.8 copy-start.2
  238.0 2.5 %copy-start.1 = (f32[48,1536]{1,0:T(8,128)S(1)}, f32[48,1536]{1,0:T(8,128)}, u32[]{:S(2)}) copy-start(f32[48,1536]{1,0:T(8,128)} %get-tuple-element.71) | copy-start | bytes 884740

commit v2 on v0

--- a/solution.py
+++ b/solution.py
@@ -3,6 +3,8 @@
 import jax
 import jax.numpy as jnp
 from jax import lax
+from jax.experimental import pallas as pl
+from jax.experimental.pallas import tpu as pltpu
 from jax.sharding import PartitionSpec as P
 
 HEAD_DIM = 64
@@ -12,6 +14,8 @@
 SCALE = 0.125
 NEGATIVE = -1000000000.0
 TILE = 512
+GELU_A = 0.7978845608028654
+GELU_B = 0.044715
 
 
 def contract_rows(left, right):
@@ -457,9 +461,1089 @@
     )
 
 
+MESH = pl.DeviceIdType.MESH
+VMEM_BYTES = 67043328
+PIECES = 4
+
+
+def dot_nn(left, right):
+    return lax.dot_general(
+        left, right, (((1,), (0,)), ((), ())), preferred_element_type=jnp.float32
+    )
+
+
+def dot_nt(left, right):
+    return lax.dot_general(
+        left, right, (((1,), (1,)), ((), ())), preferred_element_type=jnp.float32
+    )
+
+
+def remote(source, target, send, receive, device):
+    return pltpu.make_async_remote_copy(
+        src_ref=source,
+        dst_ref=target,
+        send_sem=send,
+        recv_sem=receive,
+        device_id=device,
+        device_id_type=MESH,
+    )
+
+
+def aligned(index, size, unit=16):
+    return pl.ds(pl.multiple_of(index * size, unit), size)
+
+
+class Place:
+    def __init__(self, line):
+        self.line = line
+        self.f = lax.axis_index("fsdp")
+        self.c = lax.axis_index("ctx")
+        self.t = lax.axis_index("tp")
+        self.core_bit = lax.rem(self.c, 2)
+        self.row_bit = self.c // 2
+        self.core = self.c + 1 - 2 * self.core_bit
+        self.row = lax.rem(self.c + 2, 4)
+        self.other = lax.rem(self.core + 2, 4)
+        self.core_device = (self.f, self.core, self.t)
+        self.row_device = (self.f, self.row, self.t)
+        self.tp_device = (self.f, self.c, 1 - self.t)
+
+    def line_device(self, f):
+        return (f, self.c, self.t)
+
+    def greet(self):
+        barrier = pltpu.get_barrier_semaphore()
+        others = [self.core_device, self.row_device, self.tp_device]
+        for step in range(1, self.line):
+            others.append(self.line_device(lax.rem(self.f + step, self.line)))
+        for device in others:
+            pl.semaphore_signal(barrier, 1, device_id=device, device_id_type=MESH)
+        pl.semaphore_wait(barrier, len(others))
+
+    def each(self, step, action):
+        if step == 0:
+            action(self.f, 0)
+            return
+
+        @pl.when(self.f - step >= 0)
+        def _():
+            action(self.f - step, 1)
+
+        @pl.when(self.f + step < self.line)
+        def _():
+            action(self.f + step, -1)
+
+    def can_pass(self, way):
+        return self.f < self.line - 1 if way > 0 else self.f > 0
+
+
+class Gather:
+    def __init__(self, place, group, own, full, row_first, sems):
+        self.at, self.group, self.own, self.full, self.row_first = place, group, own, full, row_first
+        self.line_send, self.line_recv, self.row_send, self.row_recv, self.core_send, self.core_recv = sems
+        self.shard = own.shape[0]
+
+    def part(self, f, other):
+        ctx = self.at.row if other else self.at.c
+        return self.full.at[aligned(f * 4 + ctx, self.shard), :]
+
+    def line_copy(self, f, way, other=0, own=False):
+        part = self.part(f, other)
+        return remote(
+            self.own if own else part,
+            part,
+            self.line_send.at[self.group, other, (way + 1) // 2, f],
+            self.line_recv.at[self.group, other, f],
+            self.at.line_device(self.at.f + way),
+        )
+
+    def row_copy(self, f, own=False):
+        part = self.part(f, 0)
+        return remote(
+            self.own if own else part,
+            part,
+            self.row_send.at[self.group, f],
+            self.row_recv.at[self.group, f],
+            self.at.row_device,
+        )
+
+    def core_copy(self, f, other, own=False):
+        part = self.part(f, other)
+        return remote(
+            self.own if own else part,
+            part,
+            self.core_send.at[self.group, other, f],
+            self.core_recv.at[self.group, other, f],
+            self.at.core_device,
+        )
+
+    def start_line(self, other=0):
+        for way in (1, -1):
+
+            @pl.when(self.at.can_pass(way))
+            def _(way=way):
+                self.line_copy(self.at.f, way, other, own=not other).start()
+
+    def start_row(self):
+        self.row_copy(self.at.f, own=True).start()
+
+    def start_core(self):
+        self.core_copy(self.at.f, 0, own=True).start()
+        self.full[aligned(self.at.f * 4 + self.at.c, self.shard), :] = self.own[...]
+
+    def line_step(self, step, other=0):
+        def arrive(f, way):
+            self.line_copy(f, 1, other).wait_recv()
+
+            @pl.when(self.at.can_pass(way))
+            def _():
+                self.line_copy(f, way, other).start()
+
+            self.core_copy(f, other).start()
+            if not self.row_first:
+                self.row_copy(f).start()
+
+        self.at.each(step, arrive)
+
+    def row_step(self, step):
+        def arrive(f, _):
+            self.row_copy(f).wait_recv()
+            self.core_copy(f, 1).start()
+            if self.row_first:
+                self.start_line(1)
+
+        self.at.each(step, arrive)
+
+    def finish(self):
+        for f in range(self.at.line):
+            for other in (0, 1):
+                self.core_copy(f, other).wait_recv()
+
+    def drain(self):
+        for step in range(self.at.line):
+            for way in (1, -1):
+                source = self.at.f - step * way
+                passed = (source >= 0) & (source < self.at.line) & self.at.can_pass(way)
+
+                @pl.when(passed)
+                def _(source=source, way=way):
+                    for other in range(2 if self.row_first else 1):
+                        self.line_copy(source, way, other).wait_send()
+
+        if self.row_first:
+            self.row_copy(self.at.f).wait_send()
+        for f in range(self.at.line):
+            if not self.row_first:
+                self.row_copy(f).wait_send()
+            for other in (0, 1):
+                self.core_copy(f, other).wait_send()
+
+
+class Scatter:
+    def __init__(self, place, group, shard, sems, core, row, line):
+        self.place, self.group, self.shard = place, group, shard
+        self.core_send, self.core_recv, self.row_send, self.row_recv, self.line_send, self.line_recv = sems
+        self.core, self.row, self.line = core, row, line
+
+    def core_copies(self):
+        full, landed, _ = self.core
+        at = self.place
+        copies = []
+        for f in range(at.line):
+            for y in range(2):
+                index = f * 2 + y
+                copies.append(
+                    remote(
+                        full.at[aligned(f * 4 + 2 * y + 1 - at.core_bit, self.shard), :],
+                        landed.at[pl.ds(index * self.shard, self.shard), :],
+                        self.core_send.at[self.group, index],
+                        self.core_recv.at[self.group, index],
+                        at.core_device,
+                    )
+                )
+        return copies
+
+    def row_copies(self):
+        summed, landed, _ = self.row
+        at = self.place
+        return [
+            remote(
+                summed.at[aligned(f * 2 + 1 - at.row_bit, self.shard), :],
+                landed.at[pl.ds(f * self.shard, self.shard), :],
+                self.row_send.at[self.group, f],
+                self.row_recv.at[self.group, f],
+                at.row_device,
+            )
+            for f in range(at.line)
+        ]
+
+    def line_copies(self):
+        summed, landed, _ = self.line
+        at = self.place
+        copies = []
+        for step in range(1, at.line):
+            target = lax.rem(at.f + step, at.line)
+            copies.append(
+                remote(
+                    summed.at[aligned(target, self.shard), :],
+                    landed.at[pl.ds((step - 1) * self.shard, self.shard), :],
+                    self.line_send.at[self.group, step],
+                    self.line_recv.at[self.group, step],
+                    at.line_device(target),
+                )
+            )
+        return copies
+
+    def start(self, stage):
+        for copy in getattr(self, stage + "_copies")():
+            copy.start()
+
+    def core_finish(self):
+        full, landed, summed = self.core
+        at = self.place
+        for index, copy in enumerate(self.core_copies()):
+            copy.wait_recv()
+            f, y = index // 2, index % 2
+            own = full[aligned(f * 4 + 2 * y + at.core_bit, self.shard), :]
+            other = landed[index * self.shard : (index + 1) * self.shard, :]
+            summed[index * self.shard : (index + 1) * self.shard, :] = (
+                own.astype(jnp.float32) + other.astype(jnp.float32)
+            ).astype(summed.dtype)
+
+    def row_finish(self):
+        summed, landed, result = self.row
+        at = self.place
+        for f, copy in enumerate(self.row_copies()):
+            copy.wait_recv()
+            own = summed[aligned(f * 2 + at.row_bit, self.shard), :]
+            other = landed[f * self.shard : (f + 1) * self.shard, :]
+            result[f * self.shard : (f + 1) * self.shard, :] = (
+                own.astype(jnp.float32) + other.astype(jnp.float32)
+            ).astype(result.dtype)
+
+    def line_finish(self):
+        summed, landed, result = self.line
+        at = self.place
+        total = summed[aligned(at.f, self.shard), :].astype(jnp.float32)
+        for step, copy in enumerate(self.line_copies()):
+            copy.wait_recv()
+            total = total + landed[step * self.shard : (step + 1) * self.shard, :].astype(jnp.float32)
+        result[...] = total
+
+    def drain(self, *stages):
+        for stage in stages:
+            for copy in getattr(self, stage + "_copies")():
+                copy.wait_send()
+
+
+def split_heads(source, store, scale):
+    rows, width = source.shape
+    for pair in range(width // 128):
+        both = source[:, pair * 128 : (pair + 1) * 128].astype(jnp.float32) * scale
+        head = lax.broadcasted_iota(jnp.int32, both.shape, 1) // HEAD_DIM
+        for side in range(2):
+            store[pair, side * rows : (side + 1) * rows, :] = jnp.where(
+                head == side, both, 0.0
+            ).astype(jnp.bfloat16)
+
+
+def write_mask(r, at, key_slot, half):
+    keys = aligned(key_slot, half)
+    key_seg = r.seg[:, aligned(key_slot, half, 128)].astype(jnp.float32)
+    key_part = jnp.broadcast_to(key_seg, (128, half)).T
+    key_full = jnp.concatenate([key_part] * (half // 128), axis=1)
+    shape = (half, half)
+    key_place = r.order[0, key_slot] * half + lax.broadcasted_iota(jnp.int32, shape, 0)
+    for part in range(2):
+        query_slot = at.c * 2 + part
+        query_seg = r.seg[:, aligned(query_slot, half, 128)].astype(jnp.float32)
+        query_place = r.order[0, query_slot] * half + lax.broadcasted_iota(jnp.int32, shape, 1)
+        allowed = (key_full == query_seg) & (key_place <= query_place)
+        r.mask[keys, part * half : (part + 1) * half] = jnp.where(allowed, 0.0, NEGATIVE)
+
+
+def attend_tile(r, slot, half, rows, width):
+    keys = aligned(slot, half)
+    mask = r.mask[keys, :]
+    mask = jnp.concatenate([mask, mask], axis=1)
+    for pair in range(width // 128):
+        span = slice(pair * 128, (pair + 1) * 128)
+        scores = dot_nt(r.kv[keys, span], r.heads[pair]) + mask
+        before = r.top[pair : pair + 1, :]
+        after = jnp.maximum(before, jnp.max(scores, axis=0, keepdims=True))
+        raised = jnp.exp(scores - after)
+        fade = jnp.exp(before - after)
+        r.top[pair : pair + 1, :] = after
+        r.total[pair : pair + 1, :] = r.total[pair : pair + 1, :] * fade + jnp.sum(
+            raised, axis=0, keepdims=True
+        )
+        value = r.kv[keys, width + pair * 128 : width + (pair + 1) * 128].T
+        step = dot_nn(value, raised.astype(jnp.bfloat16))
+        for side in range(2):
+            spot = slice((2 * pair + side) * HEAD_DIM, (2 * pair + side + 1) * HEAD_DIM)
+            columns = slice(side * rows, (side + 1) * rows)
+            r.mixed[spot, :] = (
+                r.mixed[spot, :] * fade[:, columns]
+                + step[side * HEAD_DIM : (side + 1) * HEAD_DIM, columns]
+            )
+
+
+def attend_finish(r, rows, width):
+    for pair in range(width // 128):
+        for side in range(2):
+            spot = slice((2 * pair + side) * HEAD_DIM, (2 * pair + side + 1) * HEAD_DIM)
+            columns = slice(side * rows, (side + 1) * rows)
+            r.mixed[spot, :] = r.mixed[spot, :] / r.total[pair : pair + 1, columns]
+        span = slice(pair * 128, (pair + 1) * 128)
+        r.att[:, span] = r.mixed[span, :].T.astype(jnp.bfloat16)
+    r.top[...] = r.top[...] + jnp.log(r.total[...])
+
+
+def back_begin(r, rows, width):
+    split_heads(r.att_slope, r.slopes, 1.0)
+    for pair in range(width // 128):
+        span = slice(pair * 128, (pair + 1) * 128)
+        product = r.att_slope[:, span].astype(jnp.float32).T * r.mixed[span, :]
+        for side in range(2):
+            r.pull[pair : pair + 1, side * rows : (side + 1) * rows] = jnp.sum(
+                product[side * HEAD_DIM : (side + 1) * HEAD_DIM, :], axis=0, keepdims=True
+            )
+    r.dq_sum[...] = jnp.zeros_like(r.dq_sum)
+
+
+def back_tile(r, slot, target, half, rows, width):
+    keys = aligned(slot, half)
+    mask = r.mask[keys, :]
+    mask = jnp.concatenate([mask, mask], axis=1)
+    for pair in range(width // 128):
+        span = slice(pair * 128, (pair + 1) * 128)
+        value_span = slice(width + pair * 128, width + (pair + 1) * 128)
+        key = r.kv[keys, span]
+        scores = dot_nt(key, r.heads[pair]) + mask
+        chance = jnp.exp(scores - r.top[pair : pair + 1, :])
+        pulled = dot_nt(r.kv[keys, value_span], r.slopes[pair])
+        slope = (chance * (pulled - r.pull[pair : pair + 1, :])).astype(jnp.bfloat16)
+        target[:, value_span] = dot_nn(chance.astype(jnp.bfloat16), r.slopes[pair]).astype(
+            jnp.bfloat16
+        )
+        target[:, span] = dot_nn(slope, r.heads[pair]).astype(jnp.bfloat16)
+        step = dot_nn(key.T, slope)
+        for side in range(2):
+            spot = slice((2 * pair + side) * HEAD_DIM, (2 * pair + side + 1) * HEAD_DIM)
+            r.dq_sum[spot, :] += step[
+                side * HEAD_DIM : (side + 1) * HEAD_DIM, side * rows : (side + 1) * rows
+            ]
+
+
+def gelu_both(v):
+    square = v * v
+    inner = GELU_A * v * (1.0 + GELU_B * square)
+    bent = jnp.tanh(inner)
+    lifted = 0.5 * (1.0 + bent)
+    slope = lifted + 0.5 * v * (1.0 - bent * bent) * (GELU_A * (1.0 + 3.0 * GELU_B * square))
+    return (v * lifted, slope)
+
+
+def wide(ref, these):
+    return ref[these, :].astype(jnp.float32)
+
+
+def layer_kernel(line, r):
+    at = Place(line)
+    shard = r.pv_own.shape[0]
+    rows, model = r.x.shape
+    width = r.att.shape[1]
+    hidden = r.we.shape[1]
+    half, some = rows // 2, rows // PIECES
+    low = jnp.bfloat16
+    gather_sems = (r.g_line_s, r.g_line_r, r.g_row_s, r.g_row_r, r.g_core_s, r.g_core_r)
+    scatter_sems = (r.s_core_s, r.s_core_r, r.s_row_s, r.s_row_r, r.s_line_s, r.s_line_r)
+    project_in = Gather(at, 0, r.pv_own, r.pv, False, gather_sems)
+    output_in = Gather(at, 1, r.wo_own, r.wo, False, gather_sems)
+    expand_in = Gather(at, 2, r.we_own, r.we, False, gather_sems)
+    shrink_in = Gather(at, 3, r.ws_own, r.ws, True, gather_sems)
+
+    gs, ge, gp = r.ws, r.we, r.ws.at[:, 0 : 3 * width]
+    shrink = Scatter(
+        at, 0, shard, scatter_sems, (gs, r.gs1, r.gs2), (r.gs2, r.gs3, r.gs4), (r.gs4, r.gs5, r.gs_out)
+    )
+    expand = Scatter(
+        at, 1, shard, scatter_sems, (ge, r.ge1, r.ge2), (r.ge2, r.ge3, r.ge4), (r.ge4, r.ge5, r.ge_out)
+    )
+    output = Scatter(
+        at, 2, shard, scatter_sems, (r.go, r.go1, r.go2), (r.go2, r.go3, r.go4), (r.go4, r.go5, r.go_out)
+    )
+    project = Scatter(
+        at, 3, shard, scatter_sems, (gp, r.gp1, r.gp2), (r.gp2, r.gp3, r.gp4), (r.gp4, r.gp5, r.gp_out)
+    )
+    vector = Scatter(
+        at, 4, shard, scatter_sems, (r.gv, r.gv1, r.gv2), (r.gv2, r.gv3, r.gv4), (r.gv4, r.gv5, r.gv_out)
+    )
+
+    def kv_row(part):
+        here = r.kv.at[aligned(at.c * 2 + part, half), :]
+        return remote(here, here, r.kv_s.at[0, part], r.kv_r.at[0, part], at.row_device)
+
+    def kv_core(part, other):
+        here = r.kv.at[aligned((at.row if other else at.c) * 2 + part, half), :]
+        return remote(
+            here, here, r.kv_s.at[1 + other, part], r.kv_r.at[1 + other, part], at.core_device
+        )
+
+    def tp_copy(kind, piece):
+        source, target = (
+            (r.out_send, r.out_land),
+            (r.up_send, r.up_land),
+            (r.feed, r.feed_land),
+            (r.down_send, r.down_land),
+        )[kind]
+        these = aligned(piece, some)
+        return remote(
+            source.at[these, :],
+            target.at[these, :],
+            r.tp_s.at[kind, piece],
+            r.tp_r.at[kind, piece],
+            at.tp_device,
+        )
+
+    def slopes_of(ctx, part):
+        return r.hidden.at[aligned(ctx, half), part * 2 * width : (part + 1) * 2 * width]
+
+    def back_core(far, part):
+        return remote(
+            slopes_of(at.other if far else at.core, part),
+            r.kv_land.at[pl.ds((2 * far + part) * half, half), :],
+            r.bk_s.at[far, part],
+            r.bk_r.at[far, part],
+            at.core_device,
+        )
+
+    def back_row(part):
+        these = pl.ds(part * half, half)
+        return remote(
+            r.kv_pass.at[these, :],
+            r.kv_land2.at[these, :],
+            r.bk_s.at[2, part],
+            r.bk_r.at[2, part],
+            at.row_device,
+        )
+
+    active = r.hidden.at[0:rows, :]
+    before_slope = r.hidden.at[rows : 2 * rows, :]
+
+    r.turn[...] = jnp.zeros_like(r.turn)
+    for index, ref in enumerate((r.gain1, r.shift1, r.bias_o, r.gain2, r.shift2, r.bias_s)):
+        r.turn[index : index + 1, 0:shard] = ref[...].astype(jnp.float32)[None, :]
+    for index in range(3):
+        r.pv_own[:, index * width : (index + 1) * width] = r.wp[index]
+    r.pv_own[:, 3 * width :] = r.turn[...].T[0:shard, :].astype(low)
+    r.ebias[...] = r.ebias_own[...].astype(jnp.float32)[None, :]
+    at.greet()
+    project_in.start_line()
+    project_in.start_row()
+    project_in.start_core()
+
+    @pl.loop(0, PIECES)
+    def _(piece):
+        these = aligned(piece, some)
+        r.delta[these, :] = normalize_parts(wide(r.x, these))[0]
+
+    project_in.line_step(1)
+    project_in.row_step(0)
+
+    @pl.loop(0, 2)
+    def _(slot):
+        write_mask(r, at, slot, half)
+
+    project_in.line_step(2)
+    project_in.row_step(1)
+
+    @pl.loop(2, 4)
+    def _(slot):
+        write_mask(r, at, slot, half)
+
+    for step in range(3, line):
+        project_in.line_step(step)
+        project_in.row_step(step - 1)
+    output_in.start_line()
+    output_in.start_row()
+    output_in.start_core()
+    expand_in.start_line()
+    expand_in.start_core()
+    shrink_in.start_line()
+    shrink_in.start_core()
+    project_in.row_step(line - 1)
+    project_in.finish()
+    r.vec[...] = r.pv[:, 3 * width :].astype(jnp.float32).T[0:8, :]
+    gain, shift = r.vec[0:1, :], r.vec[1:2, :]
+
+    @pl.loop(0, PIECES)
+    def _(piece):
+        these = aligned(piece, some)
+        r.normed[these, :] = (r.delta[these, :] * gain + shift).astype(low)
+
+    bias = r.pbias[...].astype(jnp.float32)
+    output_in.line_step(1)
+    for part in range(2):
+        left = r.normed[part * half : (part + 1) * half, :]
+        here = aligned(at.c * 2 + part, half)
+        r.kv[here, 0:width] = dot_nn(left, r.pv[:, width : 2 * width]).astype(low)
+        r.kv[here, width:] = (dot_nn(left, r.pv[:, 2 * width : 3 * width]) + bias[1:2, :]).astype(low)
+        kv_row(part).start()
+        kv_core(part, 0).start()
+        output_in.line_step(2 + part)
+        output_in.row_step(part)
+    shrink_in.start_row()
+    expand_in.start_row()
+    r.att[...] = (dot_nn(r.normed[...], r.pv[:, 0:width]) + bias[0:1, :]).astype(low)
+    split_heads(r.att, r.heads, SCALE)
+    r.top[...] = jnp.full_like(r.top, NEGATIVE)
+    r.total[...] = jnp.zeros_like(r.total)
+    r.mixed[...] = jnp.zeros_like(r.mixed)
+
+    @pl.loop(4, 8)
+    def _(slot):
+        write_mask(r, at, slot, half)
+
+    @pl.loop(0, 8)
+    def _(tile):
+        @pl.when(tile == 2)
+        def _():
+            for part in range(2):
+                kv_core(part, 0).wait_recv()
+            for weight in (expand_in, shrink_in):
+                weight.line_step(1)
+
+        for part in range(2):
+
+            @pl.when(tile == 4 + 2 * part)
+            def _(part=part):
+                kv_row(part).wait_recv()
+                kv_core(part, 1).start()
+                for weight in (expand_in, shrink_in):
+                    weight.line_step(2 + part)
+
+            @pl.when(tile == 5 + 2 * part)
+            def _(part=part):
+                kv_core(part, 1).wait_recv()
+
+        far = jnp.where(lax.rem(tile, 2) == 0, at.row, at.other)
+        ctx = jnp.where(tile < 2, at.c, jnp.where(tile < 4, at.core, far))
+        part = jnp.where(tile < 4, lax.rem(tile, 2), (tile - 4) // 2)
+        attend_tile(r, ctx * 2 + part, half, rows, width)
+
+    attend_finish(r, rows, width)
+    for step in range(2, line):
+        output_in.row_step(step)
+    output_in.finish()
+
+    @pl.loop(0, PIECES)
+    def _(piece):
+        these = aligned(piece, some)
+        r.out_send[these, :] = dot_nt(r.att[these, :], r.wo[...]).astype(low)
+        tp_copy(0, piece).start()
+
+    shrink_in.row_step(0)
+    for step in range(line):
+        expand_in.row_step(step)
+        if step + 1 < line:
+            shrink_in.line_step(step + 1, 1)
+    shrink_in.finish()
+    expand_in.finish()
+    out_bias, gain2, shift2 = r.vec[2:3, :], r.vec[3:4, :], r.vec[4:5, :]
+
+    @pl.loop(0, PIECES)
+    def _(piece):
+        these = aligned(piece, some)
+        tp_copy(0, piece).wait_recv()
+        middle = wide(r.x, these) + (wide(r.out_send, these) + wide(r.out_land, these)) + out_bias
+        r.mid[these, :] = middle
+        unit, _ = normalize_parts(middle)
+        normed = (unit * gain2 + shift2).astype(low)
+        r.normed2[these, :] = normed
+        for column in range(0, hidden, 512):
+            span = slice(column, column + 512)
+            value, slope = gelu_both(dot_nn(normed, r.we[:, span]) + r.ebias[:, span])
+            active[these, span] = value.astype(low)
+            before_slope[these, span] = (dot_nn(r.ct[these, :], r.ws[:, span]) * slope).astype(low)
+        r.up_send[these, :] = dot_nt(before_slope[these, :], r.we[...]).astype(low)
+        tp_copy(1, piece).start()
+
+    @pl.loop(0, PIECES)
+    def _(piece):
+        these = aligned(piece, some)
+        r.feed[these, :] = dot_nt(active[these, :], r.ws[...]).astype(low)
+        tp_copy(2, piece).start()
+
+    for weight in (shrink_in, expand_in):
+        weight.drain()
+    r.turned[...] = r.ct[...].T
+    for column in range(0, hidden, 512):
+        span = slice(column, column + 512)
+        gs[:, span] = dot_nn(r.turned[...], active[:, span]).astype(low)
+    shrink.start("core")
+    r.turned[...] = r.normed2[...].T
+    for column in range(0, hidden, 512):
+        span = slice(column, column + 512)
+        ge[:, span] = dot_nn(r.turned[...], before_slope[:, span]).astype(low)
+    expand.start("core")
+    shrink.core_finish()
+    shrink.start("row")
+    r.bsum[...] = jnp.sum(before_slope[...].astype(jnp.float32), axis=0, keepdims=True)
+    expand.core_finish()
+    expand.start("row")
+    r.vsum[...] = jnp.zeros_like(r.vsum)
+
+    @pl.loop(0, PIECES)
+    def _(piece):
+        these = aligned(piece, some)
+        tp_copy(1, piece).wait_recv()
+        upstream = wide(r.up_send, these) + wide(r.up_land, these)
+        unit, inverse = normalize_parts(r.mid[these, :])
+        back, gain_delta, shift_delta = norm_backward(upstream, unit, inverse, gain2)
+        slope = wide(r.ct, these)
+        middle_slope = slope + back
+        r.mids[these, :] = middle_slope
+        r.vsum[2:3, :] += jnp.sum(middle_slope, axis=0, keepdims=True)
+        r.vsum[3:4, :] += gain_delta[None]
+        r.vsum[4:5, :] += shift_delta[None]
+        r.vsum[5:6, :] += jnp.sum(slope, axis=0, keepdims=True)
+        rounded = middle_slope.astype(low)
+        r.normed2[these, :] = rounded
+        r.att_slope[these, :] = dot_nn(rounded, r.wo[...]).astype(low)
+
+    back_begin(r, rows, width)
+    r.turned[...] = r.normed2[...].T
+    r.go[...] = dot_nn(r.turned[...], r.att[...]).astype(low)
+    output.start("core")
+    shrink.row_finish()
+    shrink.start("line")
+
+    @pl.loop(0, 8)
+    def _(tile):
+        pair = tile // 2
+        ctx = jnp.where(
+            pair < 2, jnp.where(pair == 0, at.other, at.row), jnp.where(pair == 2, at.core, at.c)
+        )
+        part = lax.rem(tile, 2)
+        back_tile(r, ctx * 2 + part, r.tile, half, rows, width)
+        for index in range(2):
+
+            @pl.when(part == index)
+            def _(index=index):
+                slopes_of(ctx, index)[...] = r.tile[...]
+
+        for index in range(2):
+
+            @pl.when(tile == index)
+            def _(index=index):
+                back_core(1, index).start()
+
+            @pl.when(tile == 2 + index)
+            def _(index=index):
+                back_core(1, index).wait_recv()
+                landed = r.kv_land[(2 + index) * half : (3 + index) * half, :]
+                r.kv_pass[index * half : (index + 1) * half, :] = (
+                    r.tile[...].astype(jnp.float32) + landed.astype(jnp.float32)
+                ).astype(low)
+                back_row(index).start()
+
+            @pl.when(tile == 4 + index)
+            def _(index=index):
+                back_core(0, index).start()
+
+        @pl.when(tile == 3)
+        def _():
+            output.core_finish()
+            output.start("row")
+
+        @pl.when(tile == 5)
+        def _():
+            expand.row_finish()
+            expand.start("line")
+
+    for pair in range(width // 128):
+        span = slice(pair * 128, (pair + 1) * 128)
+        r.dq[:, span] = (r.dq_sum[span, :] * SCALE).T.astype(low)
+
+    @pl.loop(0, PIECES)
+    def _(piece):
+        these = aligned(piece, some)
+        r.delta[these, :] = dot_nt(r.dq[these, :], r.pv[:, 0:width])
+
+    shrink.drain("core")
+    r.turned[...] = r.normed[...].T
+    gp[:, 0:width] = dot_nn(r.turned[...], r.dq[...]).astype(low)
+    shrink_bias = r.vec[5:6, :]
+
+    @pl.loop(0, PIECES)
+    def _(piece):
+        these = aligned(piece, some)
+        tp_copy(2, piece).wait_recv()
+        feed = (wide(r.feed, these) + wide(r.feed_land, these)).astype(low)
+        r.out[these, :] = (r.mid[these, :] + feed.astype(jnp.float32) + shrink_bias).astype(low)
+
+    for part in range(2):
+        back_core(0, part).wait_recv()
+        back_row(part).wait_recv()
+        these = slice(part * half, (part + 1) * half)
+        total = slopes_of(at.c, part)[...].astype(jnp.float32)
+        total = total + wide(r.kv_land, slice(part * half, (part + 1) * half))
+        total = total + wide(r.kv_land2, these)
+        r.kv_low[these, :] = total.astype(low)
+        for step in range(PIECES // 2):
+            piece = part * (PIECES // 2) + step
+            these = slice(piece * some, (piece + 1) * some)
+            r.down_send[these, :] = (
+                r.delta[these, :] + dot_nt(r.kv_low[these, :], r.pv[:, width : 3 * width])
+            ).astype(low)
+            tp_copy(3, piece).start()
+    for piece in range(2):
+        span = slice((1 + piece) * width, (2 + piece) * width)
+        gp[:, span] = dot_nn(r.turned[...], r.kv_low[:, piece * width : (piece + 1) * width]).astype(low)
+    project.start("core")
+    bias_row = jnp.concatenate(
+        [
+            r.bsum[...],
+            jnp.sum(r.dq[...].astype(jnp.float32), axis=0, keepdims=True),
+            jnp.sum(r.kv_low[:, width:].astype(jnp.float32), axis=0, keepdims=True),
+        ],
+        axis=1,
+    )
+    r.bias_pack[...] = jnp.zeros_like(r.bias_pack)
+    for index in range(bias_row.shape[1] // 128):
+        r.bias_pack[0, index : index + 1, :] = bias_row[:, index * 128 : (index + 1) * 128]
+
+    def bias_copy(stage):
+        device = (at.core_device, at.row_device)[stage]
+        return remote(
+            r.bias_pack.at[stage], r.bias_land.at[stage], r.b_s.at[0, stage], r.b_r.at[0, stage], device
+        )
+
+    def bias_line_copy(step):
+        target = lax.rem(at.f + step, line)
+        return remote(
+            r.bias_pack.at[2],
+            r.bias_line.at[at.f],
+            r.b_s.at[1, step],
+            r.b_r.at[1, step],
+            at.line_device(target),
+        )
+
+    bias_copy(0).start()
+    output.row_finish()
+    output.start("line")
+    project.core_finish()
+    project.start("row")
+    bias_copy(0).wait_recv()
+    r.bias_pack[1, :, :] = r.bias_pack[0, :, :] + r.bias_land[0, :, :]
+    bias_copy(1).start()
+    shrink.line_finish()
+    bias_copy(1).wait_recv()
+    r.bias_pack[2, :, :] = r.bias_pack[1, :, :] + r.bias_land[1, :, :]
+    for step in range(1, line):
+        bias_line_copy(step).start()
+    project.row_finish()
+    project.start("line")
+    expand.line_finish()
+    r.turn_wide[...] = jnp.zeros_like(r.turn_wide)
+    r.turn_wide[0:8, :] = r.vsum[...]
+
+    @pl.loop(0, PIECES)
+    def _(piece):
+        these = aligned(piece, some)
+        tp_copy(3, piece).wait_recv()
+        upstream = wide(r.down_send, these) + wide(r.down_land, these)
+        unit, inverse = normalize_parts(wide(r.x, these))
+        slope, gain_delta, shift_delta = norm_backward(upstream, unit, inverse, gain)
+        r.delta[these, :] = r.mids[these, :] + slope
+        r.turn_wide[0:1, :] += gain_delta[None]
+        r.turn_wide[1:2, :] += shift_delta[None]
+
+    r.gv[...] = r.turn_wide[...].T.astype(low)
+    vector.start("core")
+    output.line_finish()
+    vector.core_finish()
+    vector.start("row")
+    vector.row_finish()
+    vector.start("line")
+    for step in range(1, line):
+        source = lax.rem(at.f + line - step, line)
+        remote(
+            r.bias_pack.at[2], r.bias_line.at[source], r.b_s.at[1, step], r.b_r.at[1, step], at.row_device
+        ).wait_recv()
+    r.bias_line[at.f, :, :] = r.bias_pack[2, :, :]
+    total = r.bias_line[0, :, :]
+    for f in range(1, line):
+        total = total + r.bias_line[f, :, :]
+    r.bias_out[...] = total
+    project.line_finish()
+    vector.line_finish()
+    project_in.drain()
+    output_in.drain()
+    for part in range(2):
+        kv_row(part).wait_send()
+        back_row(part).wait_send()
+        for index in range(2):
+            kv_core(part, index).wait_send()
+            back_core(index, part).wait_send()
+    for kind in range(4):
+        for piece in range(PIECES):
+            tp_copy(kind, piece).wait_send()
+    for stage in range(2):
+        bias_copy(stage).wait_send()
+    for step in range(1, line):
+        bias_line_copy(step).wait_send()
+    shrink.drain("row", "line")
+    for gradient in (expand, output, project, vector):
+        gradient.drain("core", "row", "line")
+
+
+def finish_kernel(r):
+    r.out_end[0] = r.out[...]
+    r.delta_end[0] = r.delta[...]
+    r.gs_end[...] = r.gs[...]
+    r.ge_end[...] = r.ge[...]
+    r.go_end[...] = r.go[...]
+    width = r.go.shape[1]
+    for index in range(3):
+        r.gp_end[index] = r.gp[:, index * width : (index + 1) * width]
+    vectors = r.gv[...].T
+    shard = r.gv.shape[0]
+    for index in range(6):
+        r["gv%d" % index][...] = vectors[index, 0:shard]
+    hidden = r.ebias.shape[0]
+    for index in range(hidden // 128):
+        r.ebias[pl.ds(index * 128, 128)] = r.biases[index, :]
+    each = width // 128
+    for index in range(2 * each):
+        row, column = index // each, index % each
+        place = hidden // 128 + index
+        r.pbias[row : row + 1, column * 128 : (column + 1) * 128] = r.biases[place : place + 1, :]
+
+
+class Refs(dict):
+    __getattr__ = dict.__getitem__
+
+
+def call(kernel, ins, outs, scratch, smem=(), identity=None):
+    names = [*ins, *outs, *scratch]
+    params = dict(vmem_limit_bytes=VMEM_BYTES)
+    if identity is not None:
+        params.update(collective_id=identity, has_side_effects=True)
+    results = pl.pallas_call(
+        lambda *refs: kernel(Refs(zip(names, refs))),
+        out_shape=[jax.ShapeDtypeStruct(shape, dtype) for shape, dtype in outs.values()],
+        in_specs=[
+            pl.BlockSpec(memory_space=pltpu.SMEM if name in smem else pltpu.VMEM) for name in ins
+        ],
+        out_specs=[pl.BlockSpec(memory_space=pltpu.VMEM)] * len(outs),
+        scratch_shapes=[
+            pltpu.VMEM(*spec) if isinstance(spec, tuple) else spec for spec in scratch.values()
+        ],
+        compiler_params=pltpu.CompilerParams(**params),
+    )(*ins.values())
+    return Refs(zip(outs, results))
+
+
+def by_kernels(
+    layer_input,
+    cotangent,
+    segments,
+    slot_order,
+    first_gain,
+    first_shift,
+    project_weight,
+    project_bias,
+    output_weight,
+    output_bias,
+    second_gain,
+    second_shift,
+    expand_weight,
+    expand_bias,
+    shrink_weight,
+    shrink_bias,
+):
+    low, full = jnp.bfloat16, jnp.float32
+    line = lax.axis_size("fsdp")
+    _, rows, model = layer_input.shape
+    length = segments.shape[1]
+    shard, _, width = project_weight.shape
+    hidden = expand_weight.shape[1]
+    pairs = width // 128
+    half = rows // 2
+    packed = 3 * width + 128
+    two, one = 2 * line * shard, line * shard
+    less = one - shard
+    bias_rows = -(-(hidden + 2 * width) // 1024) * 8
+    dma = lambda *shape: pltpu.SemaphoreType.DMA(shape)
+
+    def stages(name, columns):
+        sizes = (two, two, one, one, less)
+        return {"%s%d" % (name, index + 1): ((size, columns), low) for index, size in enumerate(sizes)}
+
+    done = call(
+        partial(layer_kernel, line),
+        dict(
+            x=layer_input.reshape(rows, model),
+            ct=cotangent.reshape(rows, model),
+            seg=segments,
+            order=slot_order,
+            gain1=first_gain,
+            shift1=first_shift,
+            bias_o=output_bias,
+            gain2=second_gain,
+            shift2=second_shift,
+            bias_s=shrink_bias,
+            wp=project_weight.transpose(1, 0, 2),
+            pbias=project_bias,
+            wo_own=output_weight.T,
+            we_own=expand_weight,
+            ws_own=shrink_weight.T,
+            ebias_own=expand_bias,
+        ),
+        dict(
+            out=((rows, model), low),
+            delta=((rows, model), full),
+            gs_out=((shard, hidden), full),
+            ge_out=((shard, hidden), full),
+            go_out=((shard, width), full),
+            gp_out=((shard, 3 * width), full),
+            gv_out=((shard, 128), full),
+            bias_out=((bias_rows, 128), full),
+        ),
+        dict(
+            pv_own=((shard, packed), low),
+            pv=((model, packed), low),
+            wo=((model, width), low),
+            we=((model, hidden), low),
+            ws=((model, hidden), low),
+            kv=((length, 2 * width), low),
+            vec=((8, model), full),
+            ebias=((1, hidden), full),
+            turn=((128, 128), full),
+            turn_wide=((128, model), full),
+            normed=((rows, model), low),
+            normed2=((rows, model), low),
+            turned=((model, rows), low),
+            mask=((length, rows), full),
+            heads=((pairs, 2 * rows, 128), low),
+            slopes=((pairs, 2 * rows, 128), low),
+            top=((8, 2 * rows), full),
+            total=((8, 2 * rows), full),
+            pull=((8, 2 * rows), full),
+            mixed=((width, rows), full),
+            dq_sum=((width, rows), full),
+            att=((rows, width), low),
+            att_slope=((rows, width), low),
+            dq=((rows, width), low),
+            tile=((half, 2 * width), low),
+            mid=((rows, model), full),
+            mids=((rows, model), full),
+            hidden=((2 * rows, hidden), low),
+            out_send=((rows, model), low),
+            out_land=((rows, model), low),
+            up_send=((rows, model), low),
+            up_land=((rows, model), low),
+            feed=((rows, model), low),
+            feed_land=((rows, model), low),
+            down_send=((rows, model), low),
+            down_land=((rows, model), low),
+            kv_land=((2 * rows, 2 * width), low),
+            kv_pass=((rows, 2 * width), low),
+            kv_land2=((rows, 2 * width), low),
+            kv_low=((rows, 2 * width), low),
+            bsum=((1, hidden), full),
+            vsum=((8, model), full),
+            go=((model, width), low),
+            gv=((model, 128), low),
+            **stages("gs", hidden),
+            **stages("ge", hidden),
+            **stages("go", width),
+            **stages("gp", 3 * width),
+            **stages("gv", 128),
+            bias_pack=((3, bias_rows, 128), full),
+            bias_land=((2, bias_rows, 128), full),
+            bias_line=((line, bias_rows, 128), full),
+            g_line_s=dma(4, 2, 2, line),
+            g_line_r=dma(4, 2, line),
+            g_row_s=dma(4, line),
+            g_row_r=dma(4, line),
+            g_core_s=dma(4, 2, line),
+            g_core_r=dma(4, 2, line),
+            s_core_s=dma(5, 2 * line),
+            s_core_r=dma(5, 2 * line),
+            s_row_s=dma(5, line),
+            s_row_r=dma(5, line),
+            s_line_s=dma(5, line),
+            s_line_r=dma(5, line),
+            kv_s=dma(3, 2),
+            kv_r=dma(3, 2),
+            tp_s=dma(4, PIECES),
+            tp_r=dma(4, PIECES),
+            bk_s=dma(3, 2),
+            bk_r=dma(3, 2),
+            b_s=dma(2, line),
+            b_r=dma(2, line),
+        ),
+        smem=("order",),
+        identity=0,
+    )
+    end = call(
+        finish_kernel,
+        dict(
+            out=done.out,
+            delta=done.delta,
+            gs=done.gs_out,
+            ge=done.ge_out,
+            go=done.go_out,
+            gp=done.gp_out,
+            gv=done.gv_out,
+            biases=done.bias_out,
+        ),
+        dict(
+            out_end=(layer_input.shape, low),
+            delta_end=(layer_input.shape, full),
+            gs_end=((shard, hidden), full),
+            ge_end=((shard, hidden), full),
+            go_end=((shard, width), full),
+            gp_end=((3, shard, width), full),
+            **{"gv%d" % index: ((shard,), full) for index in range(6)},
+            ebias=((hidden,), full),
+            pbias=((2, width), full),
+        ),
+        {},
+    )
+    return (
+        end.out_end,
+        end.delta_end,
+        end.gv0,
+        end.gv1,
+        end.gp_end.transpose(1, 0, 2),
+        end.pbias,
+        end.go_end.T,
+        end.gv2,
+        end.gv3,
+        end.gv4,
+        end.ge_end,
+        end.ebias,
+        end.gs_end.T,
+        end.gv5,
+    )
+
+
 def solution(mesh):
+    n_ctx, n_tp = mesh.shape["ctx"], mesh.shape["tp"]
+
+    def choose(layer_input, *others):
+        seqs, rows, model = layer_input.shape
+        whole_tiles = model % (16 * n_ctx * mesh.shape["fsdp"]) == 0 and rows % 256 == 0
+        if seqs == 1 and n_ctx == 4 and n_tp == 2 and whole_tiles:
+            return by_kernels(layer_input, *others)
+        return on_device(layer_input, *others)
+
     return jax.shard_map(
-        on_device,
+        choose,
         mesh=mesh,
         in_specs=(
             P("fsdp", "ctx", None),

time: 801 us -> 164 us (0.20)
  waiting for transfers between devices: 390 us -> 0 us
  blocking collectives: 167 us -> 0 us
  Pallas kernels: 0 us -> 162 us
  matrix products: 94.3 us -> 0 us
  other arithmetic: 72.5 us -> 0 us
  local copies, waits for them, and re-layouts: 52.9 us -> 0 us
  between operations: 17.1 us -> 0.82 us
    reduce_scatter x10 -> x0, waiting for transfers between devices: 215 us -> none  [the longest x1 48.6 us: on_device(): lax.psum_scatter(expand_weight_delta.astype(jnp.bfloat16), 'fsdp', scatte...]
    pallas_call x0 -> x2, Pallas kernels: none -> 162 us  [call(): pl.pallas_call(lambda *refs: kernel(Refs(zip(names, refs))), out_shape=[j...]
    dot_general x33 -> x0, matrix products: 94.3 us -> none  [the longest x6 23.5 us: masked_scores(): jnp.einsum('qhd,khd->hqk', query_heads, key_heads, preferred_element_type...]
    all_gather x5 -> x0, waiting for transfers between devices: 94.2 us -> none  [the longest x1 41 us: on_device(): lax.all_gather(expand_weight, ('fsdp', 'ctx'), axis=0, tiled=True)]
    unnamed x3 -> x0, blocking collectives: 86.8 us -> none
    psum x3 -> x0, waiting for transfers between devices: 78.4 us -> none  [the longest x1 45.2 us: on_device(): lax.psum(jnp.dot(attended_flat, output_full, preferred_element_type=jnp.f...]
    psum x1 -> x0, blocking collectives: 59.5 us -> none  [on_device(): lax.psum((project_bias_delta, expand_bias_delta), ('fsdp', 'ctx'))]
    convert_element_type x22 -> x0, other arithmetic: 36.9 us -> none  [the longest x3 19.7 us: one_item(): (chance * (pulled - jnp.sum(chance * pulled, axis=-1, keepdims=True))).as...]
  transfers between devices with their start and end apart: 18 -> 0, of which waited for: 14 -> 0; matrix products, arithmetic and copies ran while one was open for 19% -> 0% of each run, Pallas kernels for 0% -> 0%
where the time goes in v2:
time: 164 us; the launch traced here: 163 us
  Pallas kernels  162 us (99%)
    pallas_call x2, Pallas kernels, call(): pl.pallas_call(lambda *refs: kernel(Refs(zip(names, refs))), out_shape=[j...  162 us

profile of v2, /device:TPU:0, one launch (start us, length us, event | category | flops | bytes accessed | tf_op | source)
XLA Modules:
  0.0 163.2 jit_solution(17159816105149050278)
XLA Ops:
  0.7 158.7 %shard_map.263 = (bf16[512,768]{1,0:T(8,128)(2,1)}, f32[512,768]{1,0:T(8,128)}, f32[48,1536]{1,0:T(8,128)}, f32[48,1536]{1,0:T(8,128)}, f32[48,384]{1,0:T(8,128)...) custom-call(bf16[512,768]{1,0:T(8,128)(2,1)} %bitcast.8, bf16[512,768]{1,0:T(8,128)(2,1)} %bitcast.9, ...), custom_call_target="tpu_custom_call" | custom-call | tf_op jit(solution)/shard_map/pallas_call | solution.py:1334
  159.4 3.7 %shard_map.264 = (bf16[1,512,768]{2,1,0:T(8,128)(2,1)}, f32[1,512,768]{2,1,0:T(8,128)}, f32[48,1536]{1,0:T(8,128)}, f32[48,1536]{1,0:T(8,128)}, f32[48,384]{1,0:...) custom-call(bf16[512,768]{1,0:T(8,128)(2,1)} %get-tuple-element.36.r, ...), custom_call_target="tpu_custom_call" | custom-call | tf_op jit(solution)/shard_map/pallas_call | solution.py:1334

commit v3 on v2

--- a/solution.py
+++ b/solution.py
@@ -538,8 +538,9 @@
 
 
 class Gather:
-    def __init__(self, place, group, own, full, row_first, sems):
-        self.at, self.group, self.own, self.full, self.row_first = place, group, own, full, row_first
+    def __init__(self, place, group, own, full, row_first, direct, sems):
+        self.at, self.group, self.own, self.full = place, group, own, full
+        self.row_first, self.direct = row_first, direct
         self.line_send, self.line_recv, self.row_send, self.row_recv, self.core_send, self.core_recv = sems
         self.shard = own.shape[0]
 
@@ -557,6 +558,16 @@
             self.at.line_device(self.at.f + way),
         )
 
+    def direct_copy(self, step, other):
+        part = self.part(self.at.f, other)
+        return remote(
+            part if other else self.own,
+            part,
+            self.line_send.at[self.group, other, 0, step],
+            self.line_recv.at[self.group, other, self.at.f],
+            self.at.line_device(lax.rem(self.at.f + step, self.at.line)),
+        )
+
     def row_copy(self, f, own=False):
         part = self.part(f, 0)
         return remote(
@@ -578,6 +589,10 @@
         )
 
     def start_line(self, other=0):
+        if self.direct:
+            for step in range(1, self.at.line):
+                self.direct_copy(step, other).start()
+            return
         for way in (1, -1):
 
             @pl.when(self.at.can_pass(way))
@@ -594,10 +609,11 @@
     def line_step(self, step, other=0):
         def arrive(f, way):
             self.line_copy(f, 1, other).wait_recv()
-
-            @pl.when(self.at.can_pass(way))
-            def _():
-                self.line_copy(f, way, other).start()
+            if not self.direct:
+
+                @pl.when(self.at.can_pass(way))
+                def _():
+                    self.line_copy(f, way, other).start()
 
             self.core_copy(f, other).start()
             if not self.row_first:
@@ -620,7 +636,10 @@
                 self.core_copy(f, other).wait_recv()
 
     def drain(self):
-        for step in range(self.at.line):
+        for step in range(1, self.at.line if self.direct else 0):
+            for other in range(2 if self.row_first else 1):
+                self.direct_copy(step, other).wait_send()
+        for step in range(0 if self.direct else self.at.line):
             for way in (1, -1):
                 source = self.at.f - step * way
                 passed = (source >= 0) & (source < self.at.line) & self.at.can_pass(way)
@@ -640,10 +659,12 @@
 
 
 class Scatter:
-    def __init__(self, place, group, shard, sems, core, row, line):
+    def __init__(self, place, group, shard, sems, core, row, line, line_first=False):
         self.place, self.group, self.shard = place, group, shard
         self.core_send, self.core_recv, self.row_send, self.row_recv, self.line_send, self.line_recv = sems
         self.core, self.row, self.line = core, row, line
+        self.row_blocks = 1 if line_first else place.line
+        self.line_unit = 2 * shard if line_first else shard
 
     def core_copies(self):
         full, landed, _ = self.core
@@ -674,7 +695,7 @@
                 self.row_recv.at[self.group, f],
                 at.row_device,
             )
-            for f in range(at.line)
+            for f in range(self.row_blocks)
         ]
 
     def line_copies(self):
@@ -685,8 +706,8 @@
             target = lax.rem(at.f + step, at.line)
             copies.append(
                 remote(
-                    summed.at[aligned(target, self.shard), :],
-                    landed.at[pl.ds((step - 1) * self.shard, self.shard), :],
+                    summed.at[aligned(target, self.line_unit), :],
+                    landed.at[pl.ds((step - 1) * self.line_unit, self.line_unit), :],
                     self.line_send.at[self.group, step],
                     self.line_recv.at[self.group, step],
                     at.line_device(target),
@@ -724,11 +745,11 @@
     def line_finish(self):
         summed, landed, result = self.line
         at = self.place
-        total = summed[aligned(at.f, self.shard), :].astype(jnp.float32)
+        total = summed[aligned(at.f, self.line_unit), :].astype(jnp.float32)
         for step, copy in enumerate(self.line_copies()):
             copy.wait_recv()
-            total = total + landed[step * self.shard : (step + 1) * self.shard, :].astype(jnp.float32)
-        result[...] = total
+            total = total + landed[step * self.line_unit : (step + 1) * self.line_unit, :].astype(jnp.float32)
+        result[...] = total.astype(result.dtype)
 
     def drain(self, *stages):
         for stage in stages:
@@ -858,14 +879,14 @@
     low = jnp.bfloat16
     gather_sems = (r.g_line_s, r.g_line_r, r.g_row_s, r.g_row_r, r.g_core_s, r.g_core_r)
     scatter_sems = (r.s_core_s, r.s_core_r, r.s_row_s, r.s_row_r, r.s_line_s, r.s_line_r)
-    project_in = Gather(at, 0, r.pv_own, r.pv, False, gather_sems)
-    output_in = Gather(at, 1, r.wo_own, r.wo, False, gather_sems)
-    expand_in = Gather(at, 2, r.we_own, r.we, False, gather_sems)
-    shrink_in = Gather(at, 3, r.ws_own, r.ws, True, gather_sems)
-
-    gs, ge, gp = r.ws, r.we, r.ws.at[:, 0 : 3 * width]
+    project_in = Gather(at, 0, r.pv_own, r.pv, False, False, gather_sems)
+    output_in = Gather(at, 1, r.wo_own, r.wo, False, False, gather_sems)
+    expand_in = Gather(at, 2, r.we_own, r.we, False, True, gather_sems)
+    shrink_in = Gather(at, 3, r.ws_own, r.ws, True, True, gather_sems)
+
+    gs, ge = r.ws, r.we
     shrink = Scatter(
-        at, 0, shard, scatter_sems, (gs, r.gs1, r.gs2), (r.gs2, r.gs3, r.gs4), (r.gs4, r.gs5, r.gs_out)
+        at, 0, shard, scatter_sems, (gs, r.gs1, r.gs2), (r.gs4, r.gs5, r.gs_out), (r.gs2, r.gs3, r.gs4), True
     )
     expand = Scatter(
         at, 1, shard, scatter_sems, (ge, r.ge1, r.ge2), (r.ge2, r.ge3, r.ge4), (r.ge4, r.ge5, r.ge_out)
@@ -873,11 +894,23 @@
     output = Scatter(
         at, 2, shard, scatter_sems, (r.go, r.go1, r.go2), (r.go2, r.go3, r.go4), (r.go4, r.go5, r.go_out)
     )
-    project = Scatter(
-        at, 3, shard, scatter_sems, (gp, r.gp1, r.gp2), (r.gp2, r.gp3, r.gp4), (r.gp4, r.gp5, r.gp_out)
-    )
+    project = []
+    for index in range(3):
+        span = slice(index * width, (index + 1) * width)
+        landed1, summed1, landed2, summed2, landed3 = [r["gp%d%d" % (index, stage)] for stage in range(1, 6)]
+        project.append(
+            Scatter(
+                at,
+                3 + index,
+                shard,
+                scatter_sems,
+                (r.ws.at[:, span], landed1, summed1),
+                (summed1, landed2, summed2),
+                (summed2, landed3, r.gp_out.at[:, span]),
+            )
+        )
     vector = Scatter(
-        at, 4, shard, scatter_sems, (r.gv, r.gv1, r.gv2), (r.gv2, r.gv3, r.gv4), (r.gv4, r.gv5, r.gv_out)
+        at, 6, shard, scatter_sems, (r.gv, r.gv1, r.gv2), (r.gv2, r.gv3, r.gv4), (r.gv4, r.gv5, r.gv_out)
     )
 
     def kv_row(part):
@@ -892,7 +925,7 @@
 
     def tp_copy(kind, piece):
         source, target = (
-            (r.out_send, r.out_land),
+            (r.att, r.att_land),
             (r.up_send, r.up_land),
             (r.feed, r.feed_land),
             (r.down_send, r.down_land),
@@ -906,6 +939,8 @@
             at.tp_device,
         )
 
+    wo_copy = remote(r.wo, r.wo_land, r.wo_s.at[0], r.wo_r.at[0], at.tp_device)
+
     def slopes_of(ctx, part):
         return r.hidden.at[aligned(ctx, half), part * 2 * width : (part + 1) * 2 * width]
 
@@ -939,39 +974,31 @@
     r.pv_own[:, 3 * width :] = r.turn[...].T[0:shard, :].astype(low)
     r.ebias[...] = r.ebias_own[...].astype(jnp.float32)[None, :]
     at.greet()
-    project_in.start_line()
-    project_in.start_row()
-    project_in.start_core()
+    for weight in (project_in, output_in):
+        weight.start_line()
+        weight.start_row()
+        weight.start_core()
 
     @pl.loop(0, PIECES)
     def _(piece):
         these = aligned(piece, some)
         r.delta[these, :] = normalize_parts(wide(r.x, these))[0]
 
-    project_in.line_step(1)
-    project_in.row_step(0)
-
-    @pl.loop(0, 2)
-    def _(slot):
-        write_mask(r, at, slot, half)
-
-    project_in.line_step(2)
-    project_in.row_step(1)
-
-    @pl.loop(2, 4)
-    def _(slot):
-        write_mask(r, at, slot, half)
-
-    for step in range(3, line):
+    for step in range(1, line):
         project_in.line_step(step)
+        output_in.line_step(step)
+        if step == line - 2:
+            expand_in.start_line()
+            shrink_in.start_line()
         project_in.row_step(step - 1)
-    output_in.start_line()
-    output_in.start_row()
-    output_in.start_core()
-    expand_in.start_line()
+
+        if step < line - 1:
+            for slot in range(4 * step - 4, min(4 * step, 8)):
+                write_mask(r, at, slot, half)
+    shrink_in.start_row()
+    shrink_in.start_core()
+    expand_in.start_row()
     expand_in.start_core()
-    shrink_in.start_line()
-    shrink_in.start_core()
     project_in.row_step(line - 1)
     project_in.finish()
     r.vec[...] = r.pv[:, 3 * width :].astype(jnp.float32).T[0:8, :]
@@ -983,7 +1010,6 @@
         r.normed[these, :] = (r.delta[these, :] * gain + shift).astype(low)
 
     bias = r.pbias[...].astype(jnp.float32)
-    output_in.line_step(1)
     for part in range(2):
         left = r.normed[part * half : (part + 1) * half, :]
         here = aligned(at.c * 2 + part, half)
@@ -991,19 +1017,16 @@
         r.kv[here, width:] = (dot_nn(left, r.pv[:, 2 * width : 3 * width]) + bias[1:2, :]).astype(low)
         kv_row(part).start()
         kv_core(part, 0).start()
-        output_in.line_step(2 + part)
-        output_in.row_step(part)
-    shrink_in.start_row()
-    expand_in.start_row()
+    shrink_in.row_step(0)
     r.att[...] = (dot_nn(r.normed[...], r.pv[:, 0:width]) + bias[0:1, :]).astype(low)
     split_heads(r.att, r.heads, SCALE)
     r.top[...] = jnp.full_like(r.top, NEGATIVE)
     r.total[...] = jnp.zeros_like(r.total)
     r.mixed[...] = jnp.zeros_like(r.mixed)
-
-    @pl.loop(4, 8)
-    def _(slot):
-        write_mask(r, at, slot, half)
+    for step in range(line):
+        output_in.row_step(step)
+    output_in.finish()
+    wo_copy.start()
 
     @pl.loop(0, 8)
     def _(tile):
@@ -1011,8 +1034,12 @@
         def _():
             for part in range(2):
                 kv_core(part, 0).wait_recv()
-            for weight in (expand_in, shrink_in):
-                weight.line_step(1)
+
+        for step in range(1, line):
+
+            @pl.when(tile == step)
+            def _(step=step):
+                expand_in.line_step(step)
 
         for part in range(2):
 
@@ -1020,8 +1047,6 @@
             def _(part=part):
                 kv_row(part).wait_recv()
                 kv_core(part, 1).start()
-                for weight in (expand_in, shrink_in):
-                    weight.line_step(2 + part)
 
             @pl.when(tile == 5 + 2 * part)
             def _(part=part):
@@ -1033,30 +1058,24 @@
         attend_tile(r, ctx * 2 + part, half, rows, width)
 
     attend_finish(r, rows, width)
-    for step in range(2, line):
-        output_in.row_step(step)
-    output_in.finish()
-
-    @pl.loop(0, PIECES)
-    def _(piece):
-        these = aligned(piece, some)
-        r.out_send[these, :] = dot_nt(r.att[these, :], r.wo[...]).astype(low)
+    for piece in range(PIECES):
         tp_copy(0, piece).start()
-
-    shrink_in.row_step(0)
-    for step in range(line):
+    expand_in.row_step(0)
+    for step in range(1, line):
+        shrink_in.line_step(step, 0)
         expand_in.row_step(step)
-        if step + 1 < line:
-            shrink_in.line_step(step + 1, 1)
+        shrink_in.line_step(step, 1)
     shrink_in.finish()
     expand_in.finish()
+    wo_copy.wait_recv()
     out_bias, gain2, shift2 = r.vec[2:3, :], r.vec[3:4, :], r.vec[4:5, :]
 
     @pl.loop(0, PIECES)
     def _(piece):
         these = aligned(piece, some)
         tp_copy(0, piece).wait_recv()
-        middle = wide(r.x, these) + (wide(r.out_send, these) + wide(r.out_land, these)) + out_bias
+        branch = dot_nt(r.att[these, :], r.wo[...]) + dot_nt(r.att_land[these, :], r.wo_land[...])
+        middle = wide(r.x, these) + branch + out_bias
         r.mid[these, :] = middle
         unit, _ = normalize_parts(middle)
         normed = (unit * gain2 + shift2).astype(low)
@@ -1088,7 +1107,7 @@
         ge[:, span] = dot_nn(r.turned[...], before_slope[:, span]).astype(low)
     expand.start("core")
     shrink.core_finish()
-    shrink.start("row")
+    shrink.start("line")
     r.bsum[...] = jnp.sum(before_slope[...].astype(jnp.float32), axis=0, keepdims=True)
     expand.core_finish()
     expand.start("row")
@@ -1116,8 +1135,6 @@
     r.turned[...] = r.normed2[...].T
     r.go[...] = dot_nn(r.turned[...], r.att[...]).astype(low)
     output.start("core")
-    shrink.row_finish()
-    shrink.start("line")
 
     @pl.loop(0, 8)
     def _(tile):
@@ -1152,15 +1169,20 @@
             def _(index=index):
                 back_core(0, index).start()
 
-        @pl.when(tile == 3)
+        @pl.when(tile == 1)
         def _():
             output.core_finish()
             output.start("row")
 
-        @pl.when(tile == 5)
+        @pl.when(tile == 6)
         def _():
             expand.row_finish()
             expand.start("line")
+
+        @pl.when(tile == 7)
+        def _():
+            output.row_finish()
+            output.start("line")
 
     for pair in range(width // 128):
         span = slice(pair * 128, (pair + 1) * 128)
@@ -1173,7 +1195,10 @@
 
     shrink.drain("core")
     r.turned[...] = r.normed[...].T
-    gp[:, 0:width] = dot_nn(r.turned[...], r.dq[...]).astype(low)
+    r.ws[:, 0:width] = dot_nn(r.turned[...], r.dq[...]).astype(low)
+    project[0].start("core")
+    shrink.line_finish()
+    shrink.start("row")
     shrink_bias = r.vec[5:6, :]
 
     @pl.loop(0, PIECES)
@@ -1183,6 +1208,8 @@
         feed = (wide(r.feed, these) + wide(r.feed_land, these)).astype(low)
         r.out[these, :] = (r.mid[these, :] + feed.astype(jnp.float32) + shrink_bias).astype(low)
 
+    project[0].core_finish()
+    project[0].start("row")
     for part in range(2):
         back_core(0, part).wait_recv()
         back_row(part).wait_recv()
@@ -1200,8 +1227,9 @@
             tp_copy(3, piece).start()
     for piece in range(2):
         span = slice((1 + piece) * width, (2 + piece) * width)
-        gp[:, span] = dot_nn(r.turned[...], r.kv_low[:, piece * width : (piece + 1) * width]).astype(low)
-    project.start("core")
+        slopes = r.kv_low[:, piece * width : (piece + 1) * width]
+        r.ws[:, span] = dot_nn(r.turned[...], slopes).astype(low)
+        project[1 + piece].start("core")
     bias_row = jnp.concatenate(
         [
             r.bsum[...],
@@ -1231,21 +1259,23 @@
         )
 
     bias_copy(0).start()
-    output.row_finish()
-    output.start("line")
-    project.core_finish()
-    project.start("row")
+    for piece in (1, 2):
+        project[piece].core_finish()
+        project[piece].start("row")
     bias_copy(0).wait_recv()
     r.bias_pack[1, :, :] = r.bias_pack[0, :, :] + r.bias_land[0, :, :]
     bias_copy(1).start()
-    shrink.line_finish()
+    project[0].row_finish()
+    project[0].start("line")
+    shrink.row_finish()
+    expand.line_finish()
     bias_copy(1).wait_recv()
     r.bias_pack[2, :, :] = r.bias_pack[1, :, :] + r.bias_land[1, :, :]
     for step in range(1, line):
         bias_line_copy(step).start()
-    project.row_finish()
-    project.start("line")
-    expand.line_finish()
+    output.line_finish()
+    project[1].row_finish()
+    project[1].start("line")
     r.turn_wide[...] = jnp.zeros_like(r.turn_wide)
     r.turn_wide[0:8, :] = r.vsum[...]
 
@@ -1262,7 +1292,8 @@
 
     r.gv[...] = r.turn_wide[...].T.astype(low)
     vector.start("core")
-    output.line_finish()
+    project[2].row_finish()
+    project[2].start("line")
     vector.core_finish()
     vector.start("row")
     vector.row_finish()
@@ -1277,10 +1308,12 @@
     for f in range(1, line):
         total = total + r.bias_line[f, :, :]
     r.bias_out[...] = total
-    project.line_finish()
+    for piece in project:
+        piece.line_finish()
     vector.line_finish()
     project_in.drain()
     output_in.drain()
+    wo_copy.wait_send()
     for part in range(2):
         kv_row(part).wait_send()
         back_row(part).wait_send()
@@ -1295,7 +1328,7 @@
     for step in range(1, line):
         bias_line_copy(step).wait_send()
     shrink.drain("row", "line")
-    for gradient in (expand, output, project, vector):
+    for gradient in (expand, output, *project, vector):
         gradient.drain("core", "row", "line")
 
 
@@ -1378,8 +1411,7 @@
     bias_rows = -(-(hidden + 2 * width) // 1024) * 8
     dma = lambda *shape: pltpu.SemaphoreType.DMA(shape)
 
-    def stages(name, columns):
-        sizes = (two, two, one, one, less)
+    def stages(name, columns, sizes=(two, two, one, one, less)):
         return {"%s%d" % (name, index + 1): ((size, columns), low) for index, size in enumerate(sizes)}
 
     done = call(
@@ -1441,8 +1473,8 @@
             mid=((rows, model), full),
             mids=((rows, model), full),
             hidden=((2 * rows, hidden), low),
-            out_send=((rows, model), low),
-            out_land=((rows, model), low),
+            att_land=((rows, width), low),
+            wo_land=((model, width), low),
             up_send=((rows, model), low),
             up_land=((rows, model), low),
             feed=((rows, model), low),
@@ -1457,10 +1489,12 @@
             vsum=((8, model), full),
             go=((model, width), low),
             gv=((model, 128), low),
-            **stages("gs", hidden),
+            **stages("gs", hidden, (two, two, 2 * less, 2 * shard, shard)),
             **stages("ge", hidden),
             **stages("go", width),
-            **stages("gp", 3 * width),
+            **stages("gp0", width),
+            **stages("gp1", width),
+            **stages("gp2", width),
             **stages("gv", 128),
             bias_pack=((3, bias_rows, 128), full),
             bias_land=((2, bias_rows, 128), full),
@@ -1471,12 +1505,14 @@
             g_row_r=dma(4, line),
             g_core_s=dma(4, 2, line),
             g_core_r=dma(4, 2, line),
-            s_core_s=dma(5, 2 * line),
-            s_core_r=dma(5, 2 * line),
-            s_row_s=dma(5, line),
-            s_row_r=dma(5, line),
-            s_line_s=dma(5, line),
-            s_line_r=dma(5, line),
+            s_core_s=dma(7, 2 * line),
+            s_core_r=dma(7, 2 * line),
+            s_row_s=dma(7, line),
+            s_row_r=dma(7, line),
+            s_line_s=dma(7, line),
+            s_line_r=dma(7, line),
+            wo_s=dma(1),
+            wo_r=dma(1),
             kv_s=dma(3, 2),
             kv_r=dma(3, 2),
             tp_s=dma(4, PIECES),

time: 164 us -> 145 us (0.88)
  Pallas kernels: 162 us -> 144 us
    pallas_call x2, Pallas kernels: 162 us -> 144 us  [call(): pl.pallas_call(lambda *refs: kernel(Refs(zip(names, refs))), out_shape=[j...]
where the time goes in v3:
time: 145 us
  Pallas kernels  144 us (99%)
    pallas_call x2, Pallas kernels, call(): pl.pallas_call(lambda *refs: kernel(Refs(zip(names, refs))), out_shape=[j...  144 us

profile of v3, /device:TPU:0, one launch (start us, length us, event | category | flops | bytes accessed | tf_op | source)
XLA Modules:
  0.0 145.1 jit_solution(15411295191250794808)
XLA Ops:
  0.7 140.6 %shard_map.263 = (bf16[512,768]{1,0:T(8,128)(2,1)}, f32[512,768]{1,0:T(8,128)}, f32[48,1536]{1,0:T(8,128)}, f32[48,1536]{1,0:T(8,128)}, f32[48,384]{1,0:T(8,128)...) custom-call(bf16[512,768]{1,0:T(8,128)(2,1)} %bitcast.8, bf16[512,768]{1,0:T(8,128)(2,1)} %bitcast.9, ...), custom_call_target="tpu_custom_call" | custom-call | tf_op jit(solution)/shard_map/pallas_call | solution.py:1367
  141.3 3.7 %shard_map.264 = (bf16[1,512,768]{2,1,0:T(8,128)(2,1)}, f32[1,512,768]{2,1,0:T(8,128)}, f32[48,1536]{1,0:T(8,128)}, f32[48,1536]{1,0:T(8,128)}, f32[48,384]{1,0:...) custom-call(bf16[512,768]{1,0:T(8,128)(2,1)} %get-tuple-element.36.r, ...), custom_call_target="tpu_custom_call" | custom-call | tf_op jit(solution)/shard_map/pallas_call | solution.py:1367

commit v4 on v3

--- a/solution.py
+++ b/solution.py
@@ -507,13 +507,14 @@
         self.core_device = (self.f, self.core, self.t)
         self.row_device = (self.f, self.row, self.t)
         self.tp_device = (self.f, self.c, 1 - self.t)
+        self.ctx_devices = (self.core_device, self.row_device, (self.f, self.other, self.t))
 
     def line_device(self, f):
         return (f, self.c, self.t)
 
     def greet(self):
         barrier = pltpu.get_barrier_semaphore()
-        others = [self.core_device, self.row_device, self.tp_device]
+        others = [*self.ctx_devices, self.tp_device]
         for step in range(1, self.line):
             others.append(self.line_device(lax.rem(self.f + step, self.line)))
         for device in others:
@@ -757,6 +758,60 @@
                 copy.wait_send()
 
 
+class Total:
+    def __init__(self, place, group, pack, landed, lines, sems):
+        self.at, self.group, self.pack, self.landed, self.lines = place, group, pack, landed, lines
+        self.send, self.recv = sems
+
+    def ctx_copies(self):
+        return [
+            remote(
+                self.pack.at[0],
+                self.landed.at[role],
+                self.send.at[self.group, 0, role],
+                self.recv.at[self.group, 0, role],
+                device,
+            )
+            for role, device in enumerate(self.at.ctx_devices)
+        ]
+
+    def line_copy(self, step, source):
+        return remote(
+            self.pack.at[1],
+            self.lines.at[source],
+            self.send.at[self.group, 1, step],
+            self.recv.at[self.group, 1, step],
+            self.at.line_device(lax.rem(self.at.f + step, self.at.line)),
+        )
+
+    def start(self):
+        for copy in self.ctx_copies():
+            copy.start()
+
+    def pass_on(self):
+        for copy in self.ctx_copies():
+            copy.wait_recv()
+        near = self.pack[0] + self.landed[0]
+        self.pack[1] = near + (self.landed[1] + self.landed[2])
+        for step in range(1, self.at.line):
+            self.line_copy(step, self.at.f).start()
+
+    def finish(self):
+        for step in range(1, self.at.line):
+            self.line_copy(step, lax.rem(self.at.f + self.at.line - step, self.at.line)).wait_recv()
+        self.lines[self.at.f] = self.pack[1]
+        total = self.lines[0]
+        for f in range(1, self.at.line):
+            total = total + self.lines[f]
+        return total
+
+    def drain(self):
+        for copy in self.ctx_copies():
+            copy.wait_send()
+        for step in range(1, self.at.line):
+            self.line_copy(step, self.at.f).wait_send()
+
+
 def split_heads(source, store, scale):
     rows, width = source.shape
     for pair in range(width // 128):
@@ -913,6 +968,9 @@
         at, 6, shard, scatter_sems, (r.gv, r.gv1, r.gv2), (r.gv2, r.gv3, r.gv4), (r.gv4, r.gv5, r.gv_out)
     )
 
+    biases = Total(at, 0, r.bias_pack, r.bias_land, r.bias_line, (r.b_s, r.b_r))
+    gains = Total(at, 1, r.gain_pack, r.gain_land, r.gain_line, (r.b_s, r.b_r))
+
     def kv_row(part):
         here = r.kv.at[aligned(at.c * 2 + part, half), :]
         return remote(here, here, r.kv_s.at[0, part], r.kv_r.at[0, part], at.row_device)
@@ -985,8 +1043,8 @@
         r.delta[these, :] = normalize_parts(wide(r.x, these))[0]
 
     for step in range(1, line):
-        project_in.line_step(step)
-        output_in.line_step(step)
+        for weight in (project_in, output_in):
+            weight.line_step(step)
         if step == line - 2:
             expand_in.start_line()
             shrink_in.start_line()
@@ -1070,10 +1128,7 @@
     wo_copy.wait_recv()
     out_bias, gain2, shift2 = r.vec[2:3, :], r.vec[3:4, :], r.vec[4:5, :]
 
-    @pl.loop(0, PIECES)
-    def _(piece):
-        these = aligned(piece, some)
-        tp_copy(0, piece).wait_recv()
+    def feed_forward(these):
         branch = dot_nt(r.att[these, :], r.wo[...]) + dot_nt(r.att_land[these, :], r.wo_land[...])
         middle = wide(r.x, these) + branch + out_bias
         r.mid[these, :] = middle
@@ -1086,14 +1141,21 @@
             active[these, span] = value.astype(low)
             before_slope[these, span] = (dot_nn(r.ct[these, :], r.ws[:, span]) * slope).astype(low)
         r.up_send[these, :] = dot_nt(before_slope[these, :], r.we[...]).astype(low)
+
+    @pl.loop(0, PIECES // 2)
+    def _(piece):
+        tp_copy(0, piece).wait_recv()
+        feed_forward(aligned(piece, some))
         tp_copy(1, piece).start()
 
-    @pl.loop(0, PIECES)
-    def _(piece):
-        these = aligned(piece, some)
-        r.feed[these, :] = dot_nt(active[these, :], r.ws[...]).astype(low)
+    for piece in range(PIECES // 2, PIECES):
+        tp_copy(0, piece).wait_recv()
+    feed_forward(slice(half, rows))
+    for piece in range(PIECES // 2, PIECES):
+        tp_copy(1, piece).start()
+    r.feed[...] = dot_nt(active[...], r.ws[...]).astype(low)
+    for piece in range(PIECES):
         tp_copy(2, piece).start()
-
     for weight in (shrink_in, expand_in):
         weight.drain()
     r.turned[...] = r.ct[...].T
@@ -1131,6 +1193,10 @@
         r.normed2[these, :] = rounded
         r.att_slope[these, :] = dot_nn(rounded, r.wo[...]).astype(low)
 
+    r.turn_wide[...] = jnp.zeros_like(r.turn_wide)
+    r.turn_wide[0:8, :] = r.vsum[...]
+    r.gv[...] = r.turn_wide[...].T.astype(low)
+    vector.start("core")
     back_begin(r, rows, width)
     r.turned[...] = r.normed2[...].T
     r.go[...] = dot_nn(r.turned[...], r.att[...]).astype(low)
@@ -1138,11 +1204,10 @@
 
     @pl.loop(0, 8)
     def _(tile):
-        pair = tile // 2
-        ctx = jnp.where(
-            pair < 2, jnp.where(pair == 0, at.other, at.row), jnp.where(pair == 2, at.core, at.c)
-        )
-        part = lax.rem(tile, 2)
+        odd = lax.rem(tile, 2)
+        far = jnp.where(odd == 0, at.other, at.row)
+        ctx = jnp.where(tile < 4, far, jnp.where(tile < 6, at.core, at.c))
+        part = jnp.where(tile < 4, tile // 2, odd)
         back_tile(r, ctx * 2 + part, r.tile, half, rows, width)
         for index in range(2):
 
@@ -1152,11 +1217,11 @@
 
         for index in range(2):
 
-            @pl.when(tile == index)
+            @pl.when(tile == 2 * index)
             def _(index=index):
                 back_core(1, index).start()
 
-            @pl.when(tile == 2 + index)
+            @pl.when(tile == 2 * index + 1)
             def _(index=index):
                 back_core(1, index).wait_recv()
                 landed = r.kv_land[(2 + index) * half : (3 + index) * half, :]
@@ -1173,26 +1238,34 @@
         def _():
             output.core_finish()
             output.start("row")
-
-        @pl.when(tile == 6)
+            vector.core_finish()
+            vector.start("row")
+
+        @pl.when(tile == 4)
         def _():
             expand.row_finish()
             expand.start("line")
 
-        @pl.when(tile == 7)
-        def _():
-            output.row_finish()
-            output.start("line")
-
     for pair in range(width // 128):
         span = slice(pair * 128, (pair + 1) * 128)
         r.dq[:, span] = (r.dq_sum[span, :] * SCALE).T.astype(low)
 
-    @pl.loop(0, PIECES)
-    def _(piece):
-        these = aligned(piece, some)
-        r.delta[these, :] = dot_nt(r.dq[these, :], r.pv[:, 0:width])
-
+    r.delta[...] = dot_nt(r.dq[...], r.pv[:, 0:width])
+
+    def down(part):
+        back_core(0, part).wait_recv()
+        back_row(part).wait_recv()
+        these = slice(part * half, (part + 1) * half)
+        total = slopes_of(at.c, part)[...].astype(jnp.float32)
+        total = total + wide(r.kv_land, these) + wide(r.kv_land2, these)
+        r.kv_low[these, :] = total.astype(low)
+        r.down_send[these, :] = (
+            r.delta[these, :] + dot_nt(r.kv_low[these, :], r.pv[:, width : 3 * width])
+        ).astype(low)
+        for step in range(PIECES // 2):
+            tp_copy(3, part * (PIECES // 2) + step).start()
+
+    down(0)
     shrink.drain("core")
     r.turned[...] = r.normed[...].T
     r.ws[:, 0:width] = dot_nn(r.turned[...], r.dq[...]).astype(low)
@@ -1210,21 +1283,11 @@
 
     project[0].core_finish()
     project[0].start("row")
-    for part in range(2):
-        back_core(0, part).wait_recv()
-        back_row(part).wait_recv()
-        these = slice(part * half, (part + 1) * half)
-        total = slopes_of(at.c, part)[...].astype(jnp.float32)
-        total = total + wide(r.kv_land, slice(part * half, (part + 1) * half))
-        total = total + wide(r.kv_land2, these)
-        r.kv_low[these, :] = total.astype(low)
-        for step in range(PIECES // 2):
-            piece = part * (PIECES // 2) + step
-            these = slice(piece * some, (piece + 1) * some)
-            r.down_send[these, :] = (
-                r.delta[these, :] + dot_nt(r.kv_low[these, :], r.pv[:, width : 3 * width])
-            ).astype(low)
-            tp_copy(3, piece).start()
+    output.row_finish()
+    output.start("line")
+    vector.row_finish()
+    vector.start("line")
+    down(1)
     for piece in range(2):
         span = slice((1 + piece) * width, (2 + piece) * width)
         slopes = r.kv_low[:, piece * width : (piece + 1) * width]
@@ -1242,42 +1305,20 @@
     for index in range(bias_row.shape[1] // 128):
         r.bias_pack[0, index : index + 1, :] = bias_row[:, index * 128 : (index + 1) * 128]
 
-    def bias_copy(stage):
-        device = (at.core_device, at.row_device)[stage]
-        return remote(
-            r.bias_pack.at[stage], r.bias_land.at[stage], r.b_s.at[0, stage], r.b_r.at[0, stage], device
-        )
-
-    def bias_line_copy(step):
-        target = lax.rem(at.f + step, line)
-        return remote(
-            r.bias_pack.at[2],
-            r.bias_line.at[at.f],
-            r.b_s.at[1, step],
-            r.b_r.at[1, step],
-            at.line_device(target),
-        )
-
-    bias_copy(0).start()
+    biases.start()
     for piece in (1, 2):
         project[piece].core_finish()
         project[piece].start("row")
-    bias_copy(0).wait_recv()
-    r.bias_pack[1, :, :] = r.bias_pack[0, :, :] + r.bias_land[0, :, :]
-    bias_copy(1).start()
     project[0].row_finish()
     project[0].start("line")
+    biases.pass_on()
     shrink.row_finish()
     expand.line_finish()
-    bias_copy(1).wait_recv()
-    r.bias_pack[2, :, :] = r.bias_pack[1, :, :] + r.bias_land[1, :, :]
-    for step in range(1, line):
-        bias_line_copy(step).start()
     output.line_finish()
+    vector.line_finish()
     project[1].row_finish()
     project[1].start("line")
-    r.turn_wide[...] = jnp.zeros_like(r.turn_wide)
-    r.turn_wide[0:8, :] = r.vsum[...]
+    r.gain_pack[0] = jnp.zeros_like(r.gain_pack[0])
 
     @pl.loop(0, PIECES)
     def _(piece):
@@ -1287,30 +1328,20 @@
         unit, inverse = normalize_parts(wide(r.x, these))
         slope, gain_delta, shift_delta = norm_backward(upstream, unit, inverse, gain)
         r.delta[these, :] = r.mids[these, :] + slope
-        r.turn_wide[0:1, :] += gain_delta[None]
-        r.turn_wide[1:2, :] += shift_delta[None]
-
-    r.gv[...] = r.turn_wide[...].T.astype(low)
-    vector.start("core")
+        r.gain_pack[0, 0:1, :] += gain_delta[None]
+        r.gain_pack[0, 1:2, :] += shift_delta[None]
+
+    gains.start()
     project[2].row_finish()
     project[2].start("line")
-    vector.core_finish()
-    vector.start("row")
-    vector.row_finish()
-    vector.start("line")
-    for step in range(1, line):
-        source = lax.rem(at.f + line - step, line)
-        remote(
-            r.bias_pack.at[2], r.bias_line.at[source], r.b_s.at[1, step], r.b_r.at[1, step], at.row_device
-        ).wait_recv()
-    r.bias_line[at.f, :, :] = r.bias_pack[2, :, :]
-    total = r.bias_line[0, :, :]
-    for f in range(1, line):
-        total = total + r.bias_line[f, :, :]
-    r.bias_out[...] = total
+    gains.pass_on()
+    r.turn_wide[0:8, :] = jnp.zeros_like(r.vsum)
+    r.bias_out[...] = biases.finish()
     for piece in project:
         piece.line_finish()
-    vector.line_finish()
+    r.turn_wide[0:2, :] = gains.finish()
+    r.gain_full[...] = r.turn_wide[...].T
+    r.gv_out[...] = r.gv_out[...] + r.gain_full[aligned(at.f * 4 + at.c, shard), :]
     project_in.drain()
     output_in.drain()
     wo_copy.wait_send()
@@ -1323,10 +1354,8 @@
     for kind in range(4):
         for piece in range(PIECES):
             tp_copy(kind, piece).wait_send()
-    for stage in range(2):
-        bias_copy(stage).wait_send()
-    for step in range(1, line):
-        bias_line_copy(step).wait_send()
+    biases.drain()
+    gains.drain()
     shrink.drain("row", "line")
     for gradient in (expand, output, *project, vector):
         gradient.drain("core", "row", "line")
@@ -1496,15 +1525,19 @@
             **stages("gp1", width),
             **stages("gp2", width),
             **stages("gv", 128),
-            bias_pack=((3, bias_rows, 128), full),
-            bias_land=((2, bias_rows, 128), full),
+            bias_pack=((2, bias_rows, 128), full),
+            bias_land=((3, bias_rows, 128), full),
+            gain_pack=((2, 2, model), full),
+            gain_land=((3, 2, model), full),
+            gain_line=((line, 2, model), full),
+            gain_full=((model, 128), full),
             bias_line=((line, bias_rows, 128), full),
-            g_line_s=dma(4, 2, 2, line),
-            g_line_r=dma(4, 2, line),
-            g_row_s=dma(4, line),
-            g_row_r=dma(4, line),
-            g_core_s=dma(4, 2, line),
-            g_core_r=dma(4, 2, line),
+            g_line_s=dma(5, 2, 2, line),
+            g_line_r=dma(5, 2, line),
+            g_row_s=dma(5, line),
+            g_row_r=dma(5, line),
+            g_core_s=dma(5, 2, line),
+            g_core_r=dma(5, 2, line),
             s_core_s=dma(7, 2 * line),
             s_core_r=dma(7, 2 * line),
             s_row_s=dma(7, line),
@@ -1519,8 +1552,8 @@
             tp_r=dma(4, PIECES),
             bk_s=dma(3, 2),
             bk_r=dma(3, 2),
-            b_s=dma(2, line),
-            b_r=dma(2, line),
+            b_s=dma(2, 2, max(line, 3)),
+            b_r=dma(2, 2, max(line, 3)),
         ),
         smem=("order",),
         identity=0,

time: 145 us -> 144 us (level)
    pallas_call x2, Pallas kernels: 144 us -> 143 us  [call(): pl.pallas_call(lambda *refs: kernel(Refs(zip(names, refs))), out_shape=[j...]
where the time goes in v4:
time: 144 us; the launch traced here: 143 us
  Pallas kernels  143 us (99%)
    pallas_call x2, Pallas kernels, call(): pl.pallas_call(lambda *refs: kernel(Refs(zip(names, refs))), out_shape=[j...  143 us

profile of v4, /device:TPU:0, one launch (start us, length us, event | category | flops | bytes accessed | tf_op | source)
XLA Modules:
  0.0 143.4 jit_solution(2409963929458354277)
XLA Ops:
  0.7 138.9 %shard_map.263 = (bf16[512,768]{1,0:T(8,128)(2,1)}, f32[512,768]{1,0:T(8,128)}, f32[48,1536]{1,0:T(8,128)}, f32[48,1536]{1,0:T(8,128)}, f32[48,384]{1,0:T(8,128)...) custom-call(bf16[512,768]{1,0:T(8,128)(2,1)} %bitcast.8, bf16[512,768]{1,0:T(8,128)(2,1)} %bitcast.9, ...), custom_call_target="tpu_custom_call" | custom-call | tf_op jit(solution)/shard_map/pallas_call | solution.py:1396
  139.5 3.7 %shard_map.264 = (bf16[1,512,768]{2,1,0:T(8,128)(2,1)}, f32[1,512,768]{2,1,0:T(8,128)}, f32[48,1536]{1,0:T(8,128)}, f32[48,1536]{1,0:T(8,128)}, f32[48,384]{1,0:...) custom-call(bf16[512,768]{1,0:T(8,128)(2,1)} %get-tuple-element.36.r, ...), custom_call_target="tpu_custom_call" | custom-call | tf_op jit(solution)/shard_map/pallas_call | solution.py:1396
